TPU v7x, 128 devices: a whole 4x4x4 slice. The times are simulated.
128 devices in a mesh: dom: 16 (over x, y_lo, core), blk: 8 (over z, y_hi).
Axes of the slice: x: 4, y: 4 (y_hi: 2, y_lo: 2; y = y_hi * 2 + y_lo), z: 4, core: 2. Of those that a mesh axis runs over, the one named last changes fastest.
Arguments:
- positions: float32 [3, 262144], P(None, ('dom', 'blk')), may hold values from -0.5 to 0.5
- strength: float32 [3, 262144], P(None, ('dom', 'blk')), may hold values from -0.18 to 0.18
- core_radius: float32 [262144], P(('dom', 'blk')), may hold values from 0.15 to 0.3
- dye_amount: float32 [262144], P(('dom', 'blk')), may hold values from -0.18 to 0.18
- cell_fraction: float32 [3, 262144], P(None, ('dom', 'blk')), may hold values from 0 to 1
- cell_index: int32 [262144], P(('dom', 'blk')), may hold values from 0 to 127
- tile_local: int32 [262144], P(('dom', 'blk')), may hold values from 0 to 15
- owner_dom: int32 [262144, 1], P(('dom', 'blk')), may hold values from 0 to 15; in each aligned block of 2048 rows (0 to 2047, 2048 to 4095, ...) at most 640 rows name the same one
Outputs:
- velocity: float32 [3, 262144], P(None, ('dom', 'blk'))
- tile_grid: float32 [2048, 4, 128], P(('dom', 'blk'))
Inputs may be any that keep to these rules, and one draw needn't show every extreme that they name: `owner_dom`: in every block of 2048 rows of one device no value appears more than 640 times, and in some block a value appears exactly 640 times.
All inputs are finite; a program needn't handle non-finite values.
Results may differ from a plain program's by a relative error of at most 0.0003.
Values sent between devices are 32-bit elements; how exact they have to be, the bound alone decides.
A program may use at most 64 MiB of HBM per device.

v0:
```python
import math

import jax
import jax.numpy as jnp
from jax import lax
from jax.sharding import PartitionSpec as P

time_step = 0.02
move_scale = 2.0
inverse_volume = 32.0
kernel_scale = 1.0 / (4.0 * math.pi)
highest = lax.Precision.HIGHEST


def cross_product(left_vec, right_vec):
    return jnp.stack(
        [
            left_vec[1] * right_vec[2] - left_vec[2] * right_vec[1],
            left_vec[2] * right_vec[0] - left_vec[0] * right_vec[2],
            left_vec[0] * right_vec[1] - left_vec[1] * right_vec[0],
        ]
    )


def pair_sums(partial_value, source_block, target_rows):
    points = source_block[0:3]
    vortex = source_block[3:6]
    radius = source_block[6]
    source_rows = jnp.concatenate(
        [
            -2.0 * points,
            (jnp.sum(points * points, axis=0) + radius * radius)[None],
            jnp.ones_like(radius)[None],
        ],
        axis=0,
    )
    square = lax.dot_general(
        source_rows,
        target_rows,
        (((0,), (0,)), ((), ())),
        precision=highest,
        preferred_element_type=jnp.float32,
    )
    inverse = lax.rsqrt(square)
    kernel_vals = kernel_scale * inverse * inverse * inverse
    slope_vals = -3.0 * kernel_vals * inverse * inverse
    crossed = cross_product(vortex, points)
    moment_one = (points[:, None, :] * vortex[None, :, :]).reshape(9, -1)
    moment_two = (points[:, None, :] * crossed[None, :, :]).reshape(9, -1)
    first_rows = jnp.concatenate([vortex, crossed], axis=0)
    second_rows = jnp.concatenate([vortex, crossed, moment_one, moment_two], axis=0)
    first = partial_value[0] + jnp.dot(
        first_rows, kernel_vals, precision=highest, preferred_element_type=jnp.float32
    )
    second = partial_value[1] + jnp.dot(
        second_rows, slope_vals, precision=highest, preferred_element_type=jnp.float32
    )
    return (first, second)


def block_fold(running, sources, target_rows):
    overall = sources.shape[1]
    block_width = math.gcd(overall, 1024)
    blocks = sources.reshape(7, overall // block_width, block_width).transpose(1, 0, 2)

    def scan_step(partial_value, source_block):
        return (pair_sums(partial_value, source_block, target_rows), None)

    result, ignored = lax.scan(scan_step, running, blocks)
    return result


def combine(points, vortex, first, second):
    sum_kernel = first[0:3]
    velocity = cross_product(sum_kernel, points) - first[3:6]
    term_one = cross_product(sum_kernel, vortex)
    moment_one = second[6:15].reshape(3, 3, -1)
    moment_two = second[15:24].reshape(3, 3, -1)
    dot_self = jnp.sum(vortex * points, axis=0)
    mixed_one = jnp.sum(vortex[:, None, :] * moment_one, axis=0)
    mixed_two = jnp.sum(vortex[:, None, :] * moment_two, axis=0)
    term_two = (
        dot_self * (cross_product(second[0:3], points) - second[3:6])
        - cross_product(mixed_one, points)
        + mixed_two
    )
    return (velocity, term_one + term_two)


def spline_weight(distance):
    return jnp.where(
        distance < 1.0,
        1.0 - 2.5 * distance * distance + 1.5 * distance * distance * distance,
        0.5 * (2.0 - distance) * (2.0 - distance) * (1.0 - distance),
    )


def grid_place(cell_fraction, cell_index, velocity):
    cell_start = jnp.stack([cell_index % 8, cell_index // 8 % 4, cell_index // 32]).astype(
        jnp.float32
    )
    coords = cell_start + cell_fraction + move_scale * velocity
    lowest = jnp.floor(coords)
    fraction = coords - lowest
    lowest_int = lowest.astype(jnp.int32)
    base_code = lowest_int[2] % 4 * 32 + lowest_int[1] % 4 * 8 + lowest_int[0] % 8
    return (fraction, base_code)


def node_weights(fraction):
    per_axis = [
        [
            spline_weight(fraction[axis_id] + 1.0),
            spline_weight(fraction[axis_id]),
            spline_weight(1.0 - fraction[axis_id]),
            spline_weight(2.0 - fraction[axis_id]),
        ]
        for axis_id in range(3)
    ]
    weights = []
    for along_z in range(4):
        for along_y in range(4):
            for along_x in range(4):
                weights.append(per_axis[2][along_z] * per_axis[1][along_y] * per_axis[0][along_x])
    return jnp.stack(weights)


def cells_of(base_code):
    base_x = base_code % 8
    base_y = base_code // 8 % 4
    base_z = base_code // 32
    stencil_cells = []
    for along_z in range(4):
        for along_y in range(4):
            for along_x in range(4):
                stencil_cells.append(
                    (base_z + along_z - 1) % 4 * 32
                    + (base_y + along_y - 1) % 4 * 8
                    + (base_x + along_x - 1) % 8
                )
    return jnp.stack(stencil_cells)


def spread(weights, stencil_cells):
    cell_ids = jnp.arange(128, dtype=jnp.int32)[:, None]
    overall = jnp.zeros((128, weights.shape[1]), jnp.float32)
    for node in range(64):
        overall = overall + jnp.where(
            stencil_cells[node][None, :] == cell_ids, weights[node][None, :], 0.0
        )
    return overall


def pack_rows(payload, code_values, owner_ids, owner_count, capacity):
    onehot = (owner_ids[:, None] == jnp.arange(owner_count, dtype=jnp.int32)[None, :]).astype(
        jnp.int32
    )
    earlier = jnp.sum((jnp.cumsum(onehot, axis=0) - onehot) * onehot, axis=1)
    slot_index = owner_ids * capacity + earlier
    float_rows = (
        jnp.zeros((payload.shape[0], owner_count * capacity), jnp.float32)
        .at[:, slot_index]
        .set(payload)
    )
    code_rows = jnp.full((owner_count * capacity,), -1, jnp.int32).at[slot_index].set(code_values)
    return (
        float_rows.reshape(payload.shape[0], owner_count, capacity),
        code_rows.reshape(1, owner_count, capacity),
    )


def owner_deposit(values, spread_w, tile_codes, tiles_count):
    select = (tile_codes[None, :] == jnp.arange(tiles_count, dtype=jnp.int32)[:, None]).astype(
        jnp.float32
    )
    left_rows = (select[:, None, :] * values[None, :, :]).reshape(tiles_count * 4, -1)
    deposited = lax.dot_general(
        left_rows,
        spread_w,
        (((1,), (1,)), ((), ())),
        precision=highest,
        preferred_element_type=jnp.float32,
    )
    return (deposited * inverse_volume).reshape(tiles_count, 4, 128)


def on_device(
    positions, strength, core_radius, dye_amount, cell_fraction, cell_index, tile_local, owner_dom
):
    local_count = positions.shape[1]
    tiles_count = local_count // 128
    sources = jnp.concatenate([positions, strength, core_radius[None]], axis=0)
    target_rows = jnp.concatenate(
        [
            positions,
            jnp.ones_like(positions[0])[None],
            jnp.sum(positions * positions, axis=0)[None],
        ],
        axis=0,
    )
    start_sums = (
        jnp.zeros((6, local_count), jnp.float32),
        jnp.zeros((24, local_count), jnp.float32),
    )
    first, second = block_fold(
        start_sums, lax.all_gather(sources, "blk", axis=1, tiled=True), target_rows
    )
    velocity, stretch = combine(positions, strength, first, second)
    new_strength = strength + time_step * stretch
    fraction, base_code = grid_place(cell_fraction, cell_index, velocity)
    values = jnp.concatenate([new_strength, dye_amount[None]], axis=0)
    owner_ids = owner_dom[:, 0]
    owner_count = lax.axis_size("dom")
    capacity = 5 * local_count // owner_count
    code_values = tile_local * 128 + base_code
    payload = jnp.concatenate([values, node_weights(fraction)], axis=0)
    float_rows, code_rows = pack_rows(payload, code_values, owner_ids, owner_count, capacity)
    got_floats, got_codes = (
        lax.all_to_all(float_rows, "dom", split_axis=1, concat_axis=1, tiled=True),
        lax.all_to_all(code_rows, "dom", split_axis=1, concat_axis=1, tiled=True),
    )
    got_floats = got_floats.reshape(payload.shape[0], -1)
    got_codes = got_codes.reshape(-1)
    spread_w = spread(got_floats[4:68], cells_of(got_codes % 128))
    tile_grid = owner_deposit(got_floats[0:4], spread_w, got_codes // 128, tiles_count)
    return (velocity, tile_grid)


def solution(mesh):
    placed = (
        P(None, ("dom", "blk")),
        P(None, ("dom", "blk")),
        P(("dom", "blk")),
        P(("dom", "blk")),
        P(None, ("dom", "blk")),
        P(("dom", "blk")),
        P(("dom", "blk")),
        P(("dom", "blk"), None),
    )
    return jax.shard_map(
        on_device,
        mesh=mesh,
        in_specs=placed,
        out_specs=(P(None, ("dom", "blk")), P(("dom", "blk"), None, None)),
        check_vma=False,
    )
```

profile of v0, /device:TPU:25, one launch (start us, length us, event | category | flops | bytes accessed | tf_op | source)
XLA Modules:
  0.0 625.1 jit_solution(18129418941973370120)
XLA Ops:
  3.0 31.4 %all_gather.3 = f32[7,16384]{1,0:T(8,128)S(1)} all-gather(f32[7,2048]{1,0:T(8,128)S(1)} %pad_maximum_fusion.1), channel_id=1, replica_groups=mesh['dom'=16,'blk'=8] {'blk'}, dimensions={1}, use_global_device_ids=true | all-gather | bytes 516096 | tf_op jit(solution)/shard_map/all_gather | solution.py:206
  35.3 416.4 %while.13 = (s32[]{:T(128)}, f32[6,2048]{1,0:T(8,128)S(1)}, f32[24,2048]{1,0:T(8,128)S(1)}, f32[16,7,1024]{2,1,0:T(8,128)S(1)}, f32[5,2048]{1,0:T(8,128)S(1)}, /...) while((s32[]{:T(128)}, f32[6,2048]{1,0:T(8,128)S(1)}, ...), condition=%wide.region_3.4_spmd.clone, body=%wide.region_1.3_spmd.clone.sunk | while | flops 899873792 | bytes 26444100 | solution.py:69
  35.5 9.1 %fusion.518 = f32[1024,2048]{1,0:T(8,128)} fusion(f32[5,2048]{1,0:T(8,128)S(1)} %get-tuple-element.562, f32[1,1024]{1,0:T(1,128)S(1)} %fusion.517, f32[3,1024]{1,0:T(4,128)S(1)} %get-tuple-element.524, f32[5]{0:T(128)S(1)} %pad.5.clone.2), kind=kOutput, calls=%fused_computation.20.clone.1 | convolution fusion | flops 125839360 | bytes 8445972 | tf_op jit(solution)/shard_map/while/body/eval_jaxpr/dot_general | solution.py:37
  52.7 8.6 %fusion.520 = f32[24,2048]{1,0:T(8,128)S(1)} fusion(f32[24,1024]{1,0:T(8,128)S(1)} %concatenate.27, f32[1024,2048]{1,0:T(8,128)} %fusion.518, f32[24,2048]{1,0:T(8,128)S(1)} %get-tuple-element.545, pred[]{:T(512)S(6)} %compare.1206), kind=kOutput, calls=%fused_computation.11.clone.1 | convolution fusion | flops 616660992 | bytes 8880129 | tf_op jit(solution)/shard_map/while/body/eval_jaxpr/dot_general | solution.py:55
  61.5 9.1 %fusion.518 = f32[1024,2048]{1,0:T(8,128)} fusion(f32[5,2048]{1,0:T(8,128)S(1)} %get-tuple-element.562, f32[1,1024]{1,0:T(1,128)S(1)} %fusion.517, f32[3,1024]{1,0:T(4,128)S(1)} %get-tuple-element.524, f32[5]{0:T(128)S(1)} %pad.5.clone.2), kind=kOutput, calls=%fused_computation.20.clone.1 | convolution fusion | flops 125839360 | bytes 8445972 | tf_op jit(solution)/shard_map/while/body/eval_jaxpr/dot_general | solution.py:37
  78.8 8.6 %fusion.520 = f32[24,2048]{1,0:T(8,128)S(1)} fusion(f32[24,1024]{1,0:T(8,128)S(1)} %concatenate.27, f32[1024,2048]{1,0:T(8,128)} %fusion.518, f32[24,2048]{1,0:T(8,128)S(1)} %get-tuple-element.545, pred[]{:T(512)S(6)} %compare.1206), kind=kOutput, calls=%fused_computation.11.clone.1 | convolution fusion | flops 616660992 | bytes 8880129 | tf_op jit(solution)/shard_map/while/body/eval_jaxpr/dot_general | solution.py:55
  87.6 9.1 %fusion.518 = f32[1024,2048]{1,0:T(8,128)} fusion(f32[5,2048]{1,0:T(8,128)S(1)} %get-tuple-element.562, f32[1,1024]{1,0:T(1,128)S(1)} %fusion.517, f32[3,1024]{1,0:T(4,128)S(1)} %get-tuple-element.524, f32[5]{0:T(128)S(1)} %pad.5.clone.2), kind=kOutput, calls=%fused_computation.20.clone.1 | convolution fusion | flops 125839360 | bytes 8445972 | tf_op jit(solution)/shard_map/while/body/eval_jaxpr/dot_general | solution.py:37
  104.8 8.6 %fusion.520 = f32[24,2048]{1,0:T(8,128)S(1)} fusion(f32[24,1024]{1,0:T(8,128)S(1)} %concatenate.27, f32[1024,2048]{1,0:T(8,128)} %fusion.518, f32[24,2048]{1,0:T(8,128)S(1)} %get-tuple-element.545, pred[]{:T(512)S(6)} %compare.1206), kind=kOutput, calls=%fused_computation.11.clone.1 | convolution fusion | flops 616660992 | bytes 8880129 | tf_op jit(solution)/shard_map/while/body/eval_jaxpr/dot_general | solution.py:55
  113.6 9.1 %fusion.518 = f32[1024,2048]{1,0:T(8,128)} fusion(f32[5,2048]{1,0:T(8,128)S(1)} %get-tuple-element.562, f32[1,1024]{1,0:T(1,128)S(1)} %fusion.517, f32[3,1024]{1,0:T(4,128)S(1)} %get-tuple-element.524, f32[5]{0:T(128)S(1)} %pad.5.clone.2), kind=kOutput, calls=%fused_computation.20.clone.1 | convolution fusion | flops 125839360 | bytes 8445972 | tf_op jit(solution)/shard_map/while/body/eval_jaxpr/dot_general | solution.py:37
  130.8 8.6 %fusion.520 = f32[24,2048]{1,0:T(8,128)S(1)} fusion(f32[24,1024]{1,0:T(8,128)S(1)} %concatenate.27, f32[1024,2048]{1,0:T(8,128)} %fusion.518, f32[24,2048]{1,0:T(8,128)S(1)} %get-tuple-element.545, pred[]{:T(512)S(6)} %compare.1206), kind=kOutput, calls=%fused_computation.11.clone.1 | convolution fusion | flops 616660992 | bytes 8880129 | tf_op jit(solution)/shard_map/while/body/eval_jaxpr/dot_general | solution.py:55
  139.6 9.1 %fusion.518 = f32[1024,2048]{1,0:T(8,128)} fusion(f32[5,2048]{1,0:T(8,128)S(1)} %get-tuple-element.562, f32[1,1024]{1,0:T(1,128)S(1)} %fusion.517, f32[3,1024]{1,0:T(4,128)S(1)} %get-tuple-element.524, f32[5]{0:T(128)S(1)} %pad.5.clone.2), kind=kOutput, calls=%fused_computation.20.clone.1 | convolution fusion | flops 125839360 | bytes 8445972 | tf_op jit(solution)/shard_map/while/body/eval_jaxpr/dot_general | solution.py:37
  156.8 8.6 %fusion.520 = f32[24,2048]{1,0:T(8,128)S(1)} fusion(f32[24,1024]{1,0:T(8,128)S(1)} %concatenate.27, f32[1024,2048]{1,0:T(8,128)} %fusion.518, f32[24,2048]{1,0:T(8,128)S(1)} %get-tuple-element.545, pred[]{:T(512)S(6)} %compare.1206), kind=kOutput, calls=%fused_computation.11.clone.1 | convolution fusion | flops 616660992 | bytes 8880129 | tf_op jit(solution)/shard_map/while/body/eval_jaxpr/dot_general | solution.py:55
  165.6 9.1 %fusion.518 = f32[1024,2048]{1,0:T(8,128)} fusion(f32[5,2048]{1,0:T(8,128)S(1)} %get-tuple-element.562, f32[1,1024]{1,0:T(1,128)S(1)} %fusion.517, f32[3,1024]{1,0:T(4,128)S(1)} %get-tuple-element.524, f32[5]{0:T(128)S(1)} %pad.5.clone.2), kind=kOutput, calls=%fused_computation.20.clone.1 | convolution fusion | flops 125839360 | bytes 8445972 | tf_op jit(solution)/shard_map/while/body/eval_jaxpr/dot_general | solution.py:37
  182.8 8.6 %fusion.520 = f32[24,2048]{1,0:T(8,128)S(1)} fusion(f32[24,1024]{1,0:T(8,128)S(1)} %concatenate.27, f32[1024,2048]{1,0:T(8,128)} %fusion.518, f32[24,2048]{1,0:T(8,128)S(1)} %get-tuple-element.545, pred[]{:T(512)S(6)} %compare.1206), kind=kOutput, calls=%fused_computation.11.clone.1 | convolution fusion | flops 616660992 | bytes 8880129 | tf_op jit(solution)/shard_map/while/body/eval_jaxpr/dot_general | solution.py:55
  191.6 9.1 %fusion.518 = f32[1024,2048]{1,0:T(8,128)} fusion(f32[5,2048]{1,0:T(8,128)S(1)} %get-tuple-element.562, f32[1,1024]{1,0:T(1,128)S(1)} %fusion.517, f32[3,1024]{1,0:T(4,128)S(1)} %get-tuple-element.524, f32[5]{0:T(128)S(1)} %pad.5.clone.2), kind=kOutput, calls=%fused_computation.20.clone.1 | convolution fusion | flops 125839360 | bytes 8445972 | tf_op jit(solution)/shard_map/while/body/eval_jaxpr/dot_general | solution.py:37
  208.9 8.6 %fusion.520 = f32[24,2048]{1,0:T(8,128)S(1)} fusion(f32[24,1024]{1,0:T(8,128)S(1)} %concatenate.27, f32[1024,2048]{1,0:T(8,128)} %fusion.518, f32[24,2048]{1,0:T(8,128)S(1)} %get-tuple-element.545, pred[]{:T(512)S(6)} %compare.1206), kind=kOutput, calls=%fused_computation.11.clone.1 | convolution fusion | flops 616660992 | bytes 8880129 | tf_op jit(solution)/shard_map/while/body/eval_jaxpr/dot_general | solution.py:55
  217.7 9.1 %fusion.518 = f32[1024,2048]{1,0:T(8,128)} fusion(f32[5,2048]{1,0:T(8,128)S(1)} %get-tuple-element.562, f32[1,1024]{1,0:T(1,128)S(1)} %fusion.517, f32[3,1024]{1,0:T(4,128)S(1)} %get-tuple-element.524, f32[5]{0:T(128)S(1)} %pad.5.clone.2), kind=kOutput, calls=%fused_computation.20.clone.1 | convolution fusion | flops 125839360 | bytes 8445972 | tf_op jit(solution)/shard_map/while/body/eval_jaxpr/dot_general | solution.py:37
  234.9 8.6 %fusion.520 = f32[24,2048]{1,0:T(8,128)S(1)} fusion(f32[24,1024]{1,0:T(8,128)S(1)} %concatenate.27, f32[1024,2048]{1,0:T(8,128)} %fusion.518, f32[24,2048]{1,0:T(8,128)S(1)} %get-tuple-element.545, pred[]{:T(512)S(6)} %compare.1206), kind=kOutput, calls=%fused_computation.11.clone.1 | convolution fusion | flops 616660992 | bytes 8880129 | tf_op jit(solution)/shard_map/while/body/eval_jaxpr/dot_general | solution.py:55
  243.7 9.1 %fusion.518 = f32[1024,2048]{1,0:T(8,128)} fusion(f32[5,2048]{1,0:T(8,128)S(1)} %get-tuple-element.562, f32[1,1024]{1,0:T(1,128)S(1)} %fusion.517, f32[3,1024]{1,0:T(4,128)S(1)} %get-tuple-element.524, f32[5]{0:T(128)S(1)} %pad.5.clone.2), kind=kOutput, calls=%fused_computation.20.clone.1 | convolution fusion | flops 125839360 | bytes 8445972 | tf_op jit(solution)/shard_map/while/body/eval_jaxpr/dot_general | solution.py:37
  260.9 8.6 %fusion.520 = f32[24,2048]{1,0:T(8,128)S(1)} fusion(f32[24,1024]{1,0:T(8,128)S(1)} %concatenate.27, f32[1024,2048]{1,0:T(8,128)} %fusion.518, f32[24,2048]{1,0:T(8,128)S(1)} %get-tuple-element.545, pred[]{:T(512)S(6)} %compare.1206), kind=kOutput, calls=%fused_computation.11.clone.1 | convolution fusion | flops 616660992 | bytes 8880129 | tf_op jit(solution)/shard_map/while/body/eval_jaxpr/dot_general | solution.py:55
  269.7 9.1 %fusion.518 = f32[1024,2048]{1,0:T(8,128)} fusion(f32[5,2048]{1,0:T(8,128)S(1)} %get-tuple-element.562, f32[1,1024]{1,0:T(1,128)S(1)} %fusion.517, f32[3,1024]{1,0:T(4,128)S(1)} %get-tuple-element.524, f32[5]{0:T(128)S(1)} %pad.5.clone.2), kind=kOutput, calls=%fused_computation.20.clone.1 | convolution fusion | flops 125839360 | bytes 8445972 | tf_op jit(solution)/shard_map/while/body/eval_jaxpr/dot_general | solution.py:37
  295.7 9.1 %fusion.518 = f32[1024,2048]{1,0:T(8,128)} fusion(f32[5,2048]{1,0:T(8,128)S(1)} %get-tuple-element.562, f32[1,1024]{1,0:T(1,128)S(1)} %fusion.517, f32[3,1024]{1,0:T(4,128)S(1)} %get-tuple-element.524, f32[5]{0:T(128)S(1)} %pad.5.clone.2), kind=kOutput, calls=%fused_computation.20.clone.1 | convolution fusion | flops 125839360 | bytes 8445972 | tf_op jit(solution)/shard_map/while/body/eval_jaxpr/dot_general | solution.py:37
  313.0 8.6 %fusion.520 = f32[24,2048]{1,0:T(8,128)S(1)} fusion(f32[24,1024]{1,0:T(8,128)S(1)} %concatenate.27, f32[1024,2048]{1,0:T(8,128)} %fusion.518, f32[24,2048]{1,0:T(8,128)S(1)} %get-tuple-element.545, pred[]{:T(512)S(6)} %compare.1206), kind=kOutput, calls=%fused_computation.11.clone.1 | convolution fusion | flops 616660992 | bytes 8880129 | tf_op jit(solution)/shard_map/while/body/eval_jaxpr/dot_general | solution.py:55
  321.8 9.1 %fusion.518 = f32[1024,2048]{1,0:T(8,128)} fusion(f32[5,2048]{1,0:T(8,128)S(1)} %get-tuple-element.562, f32[1,1024]{1,0:T(1,128)S(1)} %fusion.517, f32[3,1024]{1,0:T(4,128)S(1)} %get-tuple-element.524, f32[5]{0:T(128)S(1)} %pad.5.clone.2), kind=kOutput, calls=%fused_computation.20.clone.1 | convolution fusion | flops 125839360 | bytes 8445972 | tf_op jit(solution)/shard_map/while/body/eval_jaxpr/dot_general | solution.py:37
  347.8 9.1 %fusion.518 = f32[1024,2048]{1,0:T(8,128)} fusion(f32[5,2048]{1,0:T(8,128)S(1)} %get-tuple-element.562, f32[1,1024]{1,0:T(1,128)S(1)} %fusion.517, f32[3,1024]{1,0:T(4,128)S(1)} %get-tuple-element.524, f32[5]{0:T(128)S(1)} %pad.5.clone.2), kind=kOutput, calls=%fused_computation.20.clone.1 | convolution fusion | flops 125839360 | bytes 8445972 | tf_op jit(solution)/shard_map/while/body/eval_jaxpr/dot_general | solution.py:37
  373.8 9.1 %fusion.518 = f32[1024,2048]{1,0:T(8,128)} fusion(f32[5,2048]{1,0:T(8,128)S(1)} %get-tuple-element.562, f32[1,1024]{1,0:T(1,128)S(1)} %fusion.517, f32[3,1024]{1,0:T(4,128)S(1)} %get-tuple-element.524, f32[5]{0:T(128)S(1)} %pad.5.clone.2), kind=kOutput, calls=%fused_computation.20.clone.1 | convolution fusion | flops 125839360 | bytes 8445972 | tf_op jit(solution)/shard_map/while/body/eval_jaxpr/dot_general | solution.py:37
  399.8 9.1 %fusion.518 = f32[1024,2048]{1,0:T(8,128)} fusion(f32[5,2048]{1,0:T(8,128)S(1)} %get-tuple-element.562, f32[1,1024]{1,0:T(1,128)S(1)} %fusion.517, f32[3,1024]{1,0:T(4,128)S(1)} %get-tuple-element.524, f32[5]{0:T(128)S(1)} %pad.5.clone.2), kind=kOutput, calls=%fused_computation.20.clone.1 | convolution fusion | flops 125839360 | bytes 8445972 | tf_op jit(solution)/shard_map/while/body/eval_jaxpr/dot_general | solution.py:37
  425.9 9.1 %fusion.518 = f32[1024,2048]{1,0:T(8,128)} fusion(f32[5,2048]{1,0:T(8,128)S(1)} %get-tuple-element.562, f32[1,1024]{1,0:T(1,128)S(1)} %fusion.517, f32[3,1024]{1,0:T(4,128)S(1)} %get-tuple-element.524, f32[5]{0:T(128)S(1)} %pad.5.clone.2), kind=kOutput, calls=%fused_computation.20.clone.1 | convolution fusion | flops 125839360 | bytes 8445972 | tf_op jit(solution)/shard_map/while/body/eval_jaxpr/dot_general | solution.py:37
  457.3 8.6 %scatter_custom_fusion = s32[10240]{0:T(1024)} fusion(s32[2048]{0:T(1024)S(1)} %bitcast.225, s32[2048]{0:T(1024)S(1)} %fusion.349, s32[]{:T(128)} %constant.772.clone.1), kind=kCustom, calls=%fused_computation.498 | custom fusion | bytes 40964 | tf_op jit(solution)/shard_map/scatter | solution.py:165
  465.9 12.0 %all-to-all-start = ((s32[1,16,640]{2,0,1:T(1,128)}), s32[1,16,640]{2,0,1:T(1,128)S(1)}, u32[]{:S(2)}, u32[]{:S(2)}) async-start(s32[1,16,640]{2,0,1:T(1,128)} %bitcast.15), calls=%async_computation | async-start | bytes 81920 | tf_op jit(solution)/shard_map/all_to_all | solution.py:220
  504.1 36.3 %all-to-all-done.1 = f32[68,16,640]{2,0,1:T(8,128)S(1)} async-done(((f32[68,16,640]{2,0,1:T(8,128)}), f32[68,16,640]{2,0,1:T(8,128)S(1)}, u32[]{:S(2)}, u32[]{:S(2)}) %all-to-all-start.1) | async-done | bytes 2785312 | tf_op jit(solution)/shard_map/all_to_all | solution.py:219
  549.6 75.4 %fusion.288 = f32[64,128]{1,0:T(8,128)} fusion(f32[64,10240]{1,0:T(8,128)S(1)} %copy-done, f32[10240]{0:T(1024)S(1)} %bitcast.154, s32[10240]{0:T(1024)} %get-tuple-element.391, f32[10240]{0:T(1024)S(1)} %bitcast.155, s32[10240]{0:T(1024)} %get-tuple-element.392, f32[10240]{0:T(1024)S(1)} %bitcast.156, s32[10240]{0:T(1024)} %get-tuple-element.393, ...), kind=kOutput, calls=%fused_computation.374 | convolution fusion | flops 1256988672 | bytes 7897088 | tf_op jit(solution)/shard_map/dot_general | solution.py:177
  (324 shorter events, 227.5 us)
Async XLA Ops:
  35.2 416.5 %copy-start.1 = (f32[3,2048]{1,0:T(4,128)S(1)}, f32[3,2048]{1,0:T(4,128)}, u32[]{:S(2)}) copy-start(f32[3,2048]{1,0:T(4,128)} %param.10) | copy-start | bytes 73732
  35.2 416.5 %copy-start.5 = (s32[2048,1]{0,1:T(1,128)S(1)}, s32[2048,1]{0,1:T(1,128)}, u32[]{:S(2)}) copy-start(s32[2048,1]{0,1:T(1,128)} %param.17) | copy-start | bytes 24580
  35.2 421.9 %copy-start.3 = (f32[3,2048]{1,0:T(4,128)S(1)}, f32[3,2048]{1,0:T(4,128)}, u32[]{:S(2)}) copy-start(f32[3,2048]{1,0:T(4,128)} %param.14) | copy-start | bytes 73732
  35.3 422.0 %copy-start.46 = (s32[2048]{0:T(1024)S(1)}, s32[2048]{0:T(1024)}, u32[]{:S(2)}) copy-start(s32[2048]{0:T(1024)} %param.16) | copy-start | bytes 24580
  35.3 442.6 %copy-start.2 = (f32[3,2048]{1,0:T(4,128)S(1)}, f32[3,2048]{1,0:T(4,128)}, u32[]{:S(2)}) copy-start(f32[3,2048]{1,0:T(4,128)} %param.11) | copy-start | bytes 73732
  35.3 443.9 %copy-start.45 = (f32[2048]{0:T(1024)S(1)}, f32[2048]{0:T(1024)}, u32[]{:S(2)}) copy-start(f32[2048]{0:T(1024)} %param.13) | copy-start | bytes 24580
  457.2 31.5 %copy-start.4 = (f32[3,2048]{1,0:T(4,128)}, f32[3,2048]{1,0:T(4,128)S(1)}, u32[]{:S(2)}) copy-start(f32[3,2048]{1,0:T(4,128)S(1)} %get-tuple-element.102) | copy-start | bytes 73732
  465.9 28.6 %all-to-all-start = ((s32[1,16,640]{2,0,1:T(1,128)}), s32[1,16,640]{2,0,1:T(1,128)S(1)}, u32[]{:S(2)}, u32[]{:S(2)}) async-start(s32[1,16,640]{2,0,1:T(1,128)} %bitcast.15), calls=%async_computation | async-start | bytes 81920 | tf_op jit(solution)/shard_map/all_to_all | solution.py:220
  494.5 45.9 %all-to-all-start.1 = ((f32[68,16,640]{2,0,1:T(8,128)}), f32[68,16,640]{2,0,1:T(8,128)S(1)}, u32[]{:S(2)}, u32[]{:S(2)}) async-start(f32[68,16,640]{2,0,1:T(8,128)} %copy.15), calls=%async_computation.1 | async-start | bytes 5898240 | tf_op jit(solution)/shard_map/all_to_all | solution.py:219
  547.0 2.2 copy-start.9
  547.0 2.2 copy-start.10
  547.0 2.2 copy-start.11
  547.0 2.2 copy-start.12
  547.0 2.2 copy-start.13
  547.0 2.2 copy-start.14
  547.1 2.2 copy-start.15
  547.1 2.2 copy-start.16
  547.1 2.2 copy-start.17
  547.1 2.2 copy-start.18
  547.1 2.2 copy-start.19
  547.1 2.2 copy-start.20
  547.1 2.2 copy-start.21
  547.1 2.2 copy-start.22
  547.1 2.2 copy-start.23
  547.1 2.2 copy-start.24
  547.2 2.2 copy-start.25
  547.2 2.2 copy-start.26
  547.2 2.2 copy-start.27
  547.2 2.2 copy-start.28
  547.2 2.2 copy-start.29
  547.2 2.2 copy-start.30
  547.2 2.2 copy-start.31
  (17 other events, 38.0 us)
where the time goes:
time: 626 us; the launch traced here: 625 us
  matrix products  481 us (77%)
  local copies, waits for them, and re-layouts  37.2 us (6%)
  waiting for transfers between devices  36.3 us (6%)
  blocking collectives  31.4 us (5%)
  other arithmetic  18.3 us (3%)
  starting transfers between devices  17.7 us (3%)
    dot_general x16, matrix products, pair_sums(): lax.dot_general(source_rows, target_rows, (((0,), (0,)), ((), ())), preci...  145 us
    dot_general x16, matrix products, pair_sums(): jnp.dot(second_rows, slope_vals, precision=highest, preferred_element_typ...  137 us
    dot_general x16, matrix products, pair_sums(): jnp.dot(first_rows, kernel_vals, precision=highest, preferred_element_typ...  124 us
    dot_general x1, matrix products, owner_deposit(): lax.dot_general(left_rows, spread_w, (((1,), (1,)), ((), ())), precision=...  75.4 us
    all_to_all x1, waiting for transfers between devices, on_device(): lax.all_to_all(float_rows, 'dom', split_axis=1, concat_axis=1, tiled=True)  36.3 us
    all_gather x1, blocking collectives, on_device(): lax.all_gather(sources, 'blk', axis=1, tiled=True)  31.4 us
  transfers between devices with their start and end apart: 2, of which 1 were waited for; matrix products, arithmetic and copies ran while one was open for 3% of the time, Pallas kernels for 0%

commit v1 on v0

v1 whole, which is shorter than its diff:
```python
import functools
import math

import jax
import jax.numpy as jnp
from jax import lax
from jax.experimental import pallas as pl
from jax.experimental.pallas import tpu as pltpu
from jax.sharding import PartitionSpec as P

MESH = pl.DeviceIdType.MESH
f32, bf16 = jnp.float32, jnp.bfloat16
kernel_scale = 1.0 / (4.0 * math.pi)


def cross_rows(u, v):
    return [u[1] * v[2] - u[2] * v[1], u[2] * v[0] - u[0] * v[2], u[0] * v[1] - u[1] * v[0]]


def split(value, parts):
    pieces = []
    for _ in range(parts):
        piece = value.astype(bf16)
        pieces.append(piece)
        value = value - piece.astype(f32)
    return pieces


def gather_kernel(n, mine_ref, all_ref, send_sems, recv_sems):
    me = lax.axis_index("blk")
    barrier = pltpu.get_barrier_semaphore()
    for step in range(1, n):
        pl.semaphore_signal(barrier, inc=1, device_id={"blk": lax.rem(me + step, n)}, device_id_type=MESH)
    pl.semaphore_wait(barrier, n - 1)
    copies = []
    for step in range(1, n):
        copy = pltpu.make_async_remote_copy(
            src_ref=mine_ref,
            dst_ref=all_ref.at[step],
            send_sem=send_sems.at[step],
            recv_sem=recv_sems.at[step],
            device_id={"blk": lax.rem(me + step, n)},
            device_id_type=MESH,
        )
        copy.start()
        copies.append(copy)
    all_ref[0] = mine_ref[...]
    for copy in copies:
        copy.wait()


def gather(block, n):
    return pl.pallas_call(
        functools.partial(gather_kernel, n),
        out_shape=jax.ShapeDtypeStruct((n,) + block.shape, f32),
        in_specs=[pl.BlockSpec(memory_space=pltpu.VMEM)],
        out_specs=pl.BlockSpec(memory_space=pltpu.VMEM),
        scratch_shapes=[pltpu.SemaphoreType.DMA((n,)), pltpu.SemaphoreType.DMA((n,))],
        compiler_params=pltpu.CompilerParams(collective_id=0, has_side_effects=True),
    )(block)


TT, ST, CH = 256, 512, 64


def pair_kernel(t_ref, s_ref, rk_ref, rg_ref, ok_ref, og_ref, vk0, vk1, vg0, vg1):
    vk, vg = (vk0, vk1), (vg0, vg1)
    count = s_ref.shape[0] // ST
    ok_ref[...] = jnp.zeros_like(ok_ref)
    og_ref[...] = jnp.zeros_like(og_ref)

    def values(targets, index, slot):
        start = pl.multiple_of(index * ST, ST)
        for row in range(0, ST, CH):
            square = jnp.dot(
                s_ref[pl.ds(pl.multiple_of(start + row, CH), CH), :], targets, preferred_element_type=f32
            )
            inverse = lax.rsqrt(square)
            second = inverse * inverse
            kern = second * inverse
            slope = kern * second
            kern_hi = kern.astype(bf16)
            slope_hi = slope.astype(bf16)
            vk[slot][row : row + CH, :] = kern_hi
            vg[slot][row : row + CH, :] = slope_hi
            vk[slot][ST + row : ST + row + CH, :] = (kern - kern_hi.astype(f32)).astype(bf16)
            vg[slot][ST + row : ST + row + CH, :] = (slope - slope_hi.astype(f32)).astype(bf16)

    def sums(at, index, slot):
        start = pl.multiple_of(index * ST, ST)
        rk = rk_ref[:, pl.ds(start, ST)]
        rg = rg_ref[:, pl.ds(start, ST)]
        ok_ref[:, pl.ds(at, TT)] += jnp.dot(
            jnp.concatenate([rk, rk], 1), vk[slot][...], preferred_element_type=f32
        )
        og_ref[:, pl.ds(at, TT)] += jnp.dot(
            jnp.concatenate([rg, rg], 1), vg[slot][...], preferred_element_type=f32
        )

    @pl.loop(0, t_ref.shape[1] // TT)
    def _(tile):
        at = pl.multiple_of(tile * TT, TT)
        targets = t_ref[:, pl.ds(at, TT)]
        values(targets, 0, 0)

        @pl.loop(0, count // 2)
        def _(pair):
            values(targets, 2 * pair + 1, 1)
            sums(at, 2 * pair, 0)
            values(targets, jnp.minimum(2 * pair + 2, count - 1), 0)
            sums(at, 2 * pair + 1, 1)


def pair_sums(targets, sources, kernel_rows, slope_rows):
    local = targets.shape[1]
    return pl.pallas_call(
        pair_kernel,
        out_shape=(
            jax.ShapeDtypeStruct((kernel_rows.shape[0], local), f32),
            jax.ShapeDtypeStruct((slope_rows.shape[0], local), f32),
        ),
        in_specs=[pl.BlockSpec(memory_space=pltpu.VMEM)] * 4,
        out_specs=(pl.BlockSpec(memory_space=pltpu.VMEM),) * 2,
        scratch_shapes=[pltpu.VMEM((2 * ST, TT), bf16)] * 4,
        compiler_params=pltpu.CompilerParams(vmem_limit_bytes=48 << 20),
    )(targets, sources, kernel_rows, slope_rows)


def spline_weight(distance):
    return jnp.where(
        distance < 1.0,
        1.0 - 2.5 * distance * distance + 1.5 * distance * distance * distance,
        0.5 * (2.0 - distance) * (2.0 - distance) * (1.0 - distance),
    )


def axis_weights(base, fraction, cells):
    local = fraction.shape[1]
    nodes = [
        spline_weight(fraction + 1.0),
        spline_weight(fraction),
        spline_weight(1.0 - fraction),
        spline_weight(2.0 - fraction),
    ]
    ids = lax.broadcasted_iota(jnp.int32, (cells, local), 0)
    total = jnp.zeros((cells, local), f32)
    for node in range(4):
        total = total + jnp.where(((base + (node - 1)) & (cells - 1)) == ids, nodes[node], 0.0)
    return total


def deposit_kernel(
    n, ok_ref, og_ref, pos_ref, str_ref, dye_ref, frac_ref, code_ref, vel_ref, grid_ref,
    part_ref, got_ref, send_sems, recv_sems,
):
    me = lax.axis_index("dom")
    barrier = pltpu.get_barrier_semaphore()
    for step in range(1, n):
        pl.semaphore_signal(barrier, inc=1, device_id={"dom": lax.rem(me + step, n)}, device_id_type=MESH)

    points = [pos_ref[i : i + 1, :] for i in range(3)]
    vortex = [str_ref[i : i + 1, :] for i in range(3)]
    first = [ok_ref[i : i + 1, :] + ok_ref[6 + i : 7 + i, :] for i in range(6)]
    second = [og_ref[i : i + 1, :] + og_ref[24 + i : 25 + i, :] for i in range(24)]
    turned = cross_rows(first[0:3], points)
    velocity = [turned[i] - first[3 + i] for i in range(3)]
    for i in range(3):
        vel_ref[i : i + 1, :] = velocity[i]
    term_one = cross_rows(first[0:3], vortex)
    dot_self = vortex[0] * points[0] + vortex[1] * points[1] + vortex[2] * points[2]
    mixed_one = [sum(vortex[k] * second[6 + 3 * k + i] for k in range(3)) for i in range(3)]
    mixed_two = [sum(vortex[k] * second[15 + 3 * k + i] for k in range(3)) for i in range(3)]
    slope_turned = cross_rows(second[0:3], points)
    mixed_turned = cross_rows(mixed_one, points)
    values = []
    for i in range(3):
        term_two = dot_self * (slope_turned[i] - second[3 + i]) - mixed_turned[i] + mixed_two[i]
        values.append((vortex[i] + 0.02 * (term_one[i] + term_two)) * 32.0)
    values.append(dye_ref[...] * 32.0)

    cell = code_ref[0:1, :]
    starts = [cell & 7, (cell >> 3) & 3, cell >> 5]
    weights = []
    for i in range(3):
        coords = starts[i].astype(f32) + frac_ref[i : i + 1, :] + 2.0 * velocity[i]
        lowest = jnp.floor(coords)
        weights.append(axis_weights(lowest.astype(jnp.int32), coords - lowest, 8 if i == 0 else 4))
    plane = [weights[2][z : z + 1, :] * weights[1][y : y + 1, :] for z in range(4) for y in range(4)]

    tile = code_ref[1:2, :]
    local = tile.shape[1]
    tiles = grid_ref.shape[0]
    ids = lax.broadcasted_iota(jnp.int32, (n * tiles, local), 0)
    onehot = jnp.where(ids == tile, 1.0, 0.0).astype(bf16)
    for c in range(4):
        spread = jnp.concatenate([weights[0] * (plane[k] * values[c]) for k in range(16)], 0)
        total = jnp.zeros((n * tiles, 128), f32)
        for piece in split(spread, 2):
            total = total + lax.dot_general(
                onehot, piece, (((1,), (1,)), ((), ())), preferred_element_type=f32
            )
        part_ref[:, :, c, :] = total.reshape(n, tiles, 128)

    pl.semaphore_wait(barrier, n - 1)
    copies = []
    for step in range(1, n):
        peer = lax.rem(me + step, n)
        copy = pltpu.make_async_remote_copy(
            src_ref=part_ref.at[peer],
            dst_ref=got_ref.at[step],
            send_sem=send_sems.at[step],
            recv_sem=recv_sems.at[step],
            device_id={"dom": peer},
            device_id_type=MESH,
        )
        copy.start()
        copies.append(copy)
    total = part_ref[me]
    for step in range(1, n):
        copies[step - 1].wait_recv()
        total = total + got_ref[step]
    grid_ref[...] = total
    for copy in copies:
        copy.wait_send()


def deposit(n, ok, og, positions, strength, dye, fraction, codes):
    local = positions.shape[1]
    tiles = local // 128
    return pl.pallas_call(
        functools.partial(deposit_kernel, n),
        out_shape=(
            jax.ShapeDtypeStruct((3, local), f32),
            jax.ShapeDtypeStruct((tiles, 4, 128), f32),
        ),
        in_specs=[pl.BlockSpec(memory_space=pltpu.VMEM)] * 7,
        out_specs=(pl.BlockSpec(memory_space=pltpu.VMEM),) * 2,
        scratch_shapes=[
            pltpu.VMEM((n, tiles, 4, 128), f32),
            pltpu.VMEM((n, tiles, 4, 128), f32),
            pltpu.SemaphoreType.DMA((n,)),
            pltpu.SemaphoreType.DMA((n,)),
        ],
        compiler_params=pltpu.CompilerParams(collective_id=1, has_side_effects=True, vmem_limit_bytes=48 << 20),
    )(ok, og, positions, strength, dye, fraction, codes)


def source_tables(blocks):
    points = [blocks[:, i].reshape(-1) for i in range(3)]
    vortex = [blocks[:, 3 + i].reshape(-1) for i in range(3)]
    radius = blocks[:, 6].reshape(-1)
    constant = points[0] * points[0] + points[1] * points[1] + points[2] * points[2] + radius * radius
    one = jnp.ones_like(radius).astype(bf16)
    rows = []
    for i in range(3):
        a, b, c = split_whole(-2.0 * points[i], 3)
        rows += [a, b, a, b, c, a, c, b]
    rows += split_whole(constant, 3) + [one] * 3 + [jnp.zeros_like(one)] * 2
    sources = jnp.stack(rows, axis=1)
    crossed = cross_rows(vortex, points)
    lead = [kernel_scale * v for v in vortex + crossed]
    slope = [-3.0 * v for v in lead]
    slope += [points[k] * slope[i] for k in range(3) for i in range(3)] + [
        points[k] * slope[3 + i] for k in range(3) for i in range(3)
    ]
    kernel_rows = jnp.stack(split_all(lead) + [jnp.zeros_like(one)] * 4)
    slope_rows = jnp.stack(split_all(slope))
    return sources, kernel_rows, slope_rows


def split_whole(value, parts):
    pieces = []
    for _ in range(parts):
        piece = lax.reduce_precision(value, 8, 7)
        pieces.append(piece.astype(bf16))
        value = value - piece
    return pieces


def split_all(rows):
    pairs = [split_whole(row, 2) for row in rows]
    return [pair[0] for pair in pairs] + [pair[1] for pair in pairs]


def target_table(positions):
    norm = positions[0] * positions[0] + positions[1] * positions[1] + positions[2] * positions[2]
    one = jnp.ones_like(norm).astype(bf16)
    rows = []
    for i in range(3):
        a, b, c = split_whole(positions[i], 3)
        rows += [a, a, b, b, a, c, b, c]
    rows += [one] * 3 + split_whole(norm, 3) + [jnp.zeros_like(one)] * 2
    return jnp.stack(rows)


def on_device(
    positions, strength, core_radius, dye_amount, cell_fraction, cell_index, tile_local, owner_dom
):
    n_dom, n_blk = lax.axis_size("dom"), lax.axis_size("blk")
    tiles = positions.shape[1] // 128
    block = jnp.concatenate([positions, strength, core_radius[None], core_radius[None]], axis=0)
    blocks = gather(block, n_blk)
    sources, kernel_rows, slope_rows = source_tables(blocks)
    ok, og = pair_sums(target_table(positions), sources, kernel_rows, slope_rows)
    codes = jnp.stack([cell_index, owner_dom[:, 0] * tiles + tile_local])
    return deposit(n_dom, ok, og, positions, strength, dye_amount[None], cell_fraction, codes)


def solution(mesh):
    both = ("dom", "blk")
    placed = (P(None, both), P(None, both), P(both), P(both), P(None, both), P(both), P(both), P(both, None))
    return jax.shard_map(
        on_device,
        mesh=mesh,
        in_specs=placed,
        out_specs=(P(None, both), P(both, None, None)),
        check_vma=False,
    )
```

time: 626 us -> 156 us (0.25)
  matrix products: 481 us -> 0 us
  Pallas kernels: 0 us -> 112 us
  waiting for transfers between devices: 36.3 us -> 0 us
  blocking collectives: 31.4 us -> 0 us
  starting transfers between devices: 17.7 us -> 0 us
  local copies, waits for them, and re-layouts: 37.2 us -> 25.6 us
    dot_general x49 -> x0, matrix products: 481 us -> none  [the longest x16 145 us: pair_sums(): lax.dot_general(source_rows, target_rows, (((0,), (0,)), ((), ())), preci...]
    pallas_call x0 -> x3, Pallas kernels: none -> 112 us  [the longest x1 83.9 us: pair_sums(): pl.pallas_call(pair_kernel, out_shape=(jax.ShapeDtypeStruct((kernel_rows....]
    all_to_all x2 -> x0, waiting for transfers between devices: 36.3 us -> none  [the longest x1 36.3 us: on_device(): lax.all_to_all(float_rows, 'dom', split_axis=1, concat_axis=1, tiled=True)]
    all_gather x1 -> x0, blocking collectives: 31.4 us -> none  [on_device(): lax.all_gather(sources, 'blk', axis=1, tiled=True)]
    another operation x1 -> x12, local copies, waits for them, and re-layouts: 0.01 us -> 24.4 us  [the longest x5 11.5 us: source_tables(): sources = jnp.stack(rows, axis=1)]
    all_to_all x2 -> x0, starting transfers between devices: 17.7 us -> none  [the longest x1 12 us: on_device(): lax.all_to_all(code_rows, 'dom', split_axis=1, concat_axis=1, tiled=True)]
    scatter x2 -> x0, local copies, waits for them, and re-layouts: 16.9 us -> none  [the longest x1 8.63 us: pack_rows(): jnp.full((owner_count * capacity,), -1, jnp.int32).at[slot_index]]
    convert_element_type x3 -> x6, other arithmetic: 0.96 us -> 10.2 us  [split_whole(): pieces.append(piece.astype(bf16))]
  transfers between devices with their start and end apart: 2 -> 0, of which waited for: 1 -> 0; matrix products, arithmetic and copies ran while one was open for 3% -> 0% of each run, Pallas kernels for 0% -> 0%
where the time goes in v1:
time: 156 us; the launch traced here: 154 us
  Pallas kernels  112 us (72%)
  local copies, waits for them, and re-layouts  25.6 us (16%)
  other arithmetic  15.4 us (10%)
    pallas_call x1, Pallas kernels, pair_sums(): pl.pallas_call(pair_kernel, out_shape=(jax.ShapeDtypeStruct((kernel_rows....  83.9 us
    pallas_call x1, Pallas kernels, gather(): pl.pallas_call(functools.partial(gather_kernel, n), out_shape=jax.ShapeDt...  14.2 us
    pallas_call x1, Pallas kernels, deposit(): pl.pallas_call(functools.partial(deposit_kernel, n), out_shape=(jax.Shape...  13.7 us
    another operation x5, local copies, waits for them, and re-layouts, source_tables(): sources = jnp.stack(rows, axis=1)  11.5 us
    convert_element_type x6, other arithmetic, split_whole(): pieces.append(piece.astype(bf16))  10.2 us
    another operation x1, local copies, waits for them, and re-layouts, source_tables(): slope_rows = jnp.stack(split_all(slope))  9.5 us
    slice x1, other arithmetic, source_tables(): points = [blocks[:, i].reshape(-1) for i in range(3)]  3.72 us

profile of v1, /device:TPU:25, one launch (start us, length us, event | category | flops | bytes accessed | tf_op | source)
XLA Modules:
  0.0 153.7 jit_solution(2264398673917383204)
XLA Ops:
  0.6 1.5 pad_maximum_fusion.mine_ref
  2.1 14.2 %shard_map.95 = f32[8,8,2048]{2,1,0:T(8,128)} custom-call(f32[8,2048]{1,0:T(8,128)} %pad_maximum_fusion.mine_ref), custom_call_target="tpu_custom_call" | custom-call | tf_op jit(solution)/shard_map/pallas_call | solution.py:53
  16.3 3.7 %fusion.76 = (f32[8,1,2048]{2,1,0:T(1,128)S(1)}, f32[8,1,2048]{2,1,0:T(1,128)}, f32[8,1,2048]{2,1,0:T(1,128)}, f32[8,1,2048]{2,1,0:T(1,128)}, f32[8,1,2048]{2,1,...) fusion(f32[8,8,2048]{2,1,0:T(8,128)} %shard_map.95), kind=kLoop, calls=%fused_computation.185 | loop fusion | flops 163840 | bytes 1114112 | tf_op jit(solution)/shard_map/slice | solution.py:249
  20.0 3.4 %fusion.67 = (bf16[1,16384]{1,0:T(2,128)(2,1)S(1)}, f32[1,16384]{1,0:T(1,128)S(1)}, bf16[1,16384]{1,0:T(2,128)(2,1)S(1)}, f32[1,16384]{1,0:T(1,128)S(1)}, bf16[1...) fusion(f32[1,16384]{1,0:T(1,128)S(1)} %bitcast.18, ...), kind=kLoop, calls=%fused_computation.143 | loop fusion | flops 1916928 | bytes 1671168 | tf_op jit(solution)/shard_map/convert_element_type | solution.py:275
  23.5 3.0 %fusion.61 = (bf16[1,16384]{1,0:T(2,128)(2,1)S(1)}, bf16[1,16384]{1,0:T(2,128)(2,1)S(1)}, bf16[1,16384]{1,0:T(2,128)(2,1)S(1)}, bf16[1,16384]{1,0:T(2,128)(2,1)}...) fusion(f32[1,16384]{1,0:T(1,128)S(1)} %bitcast.21, ...), kind=kLoop, calls=%fused_computation.137 | loop fusion | flops 1327104 | bytes 1277952 | tf_op jit(solution)/shard_map/convert_element_type | solution.py:275
  26.5 9.5 %stack.38.rg_ref = bf16[48,16384]{1,0:T(8,128)(2,1)S(1)} concatenate(bf16[1,16384]{1,0:T(2,128)(2,1)S(1)} %get-tuple-element.67, bf16[1,16384]{1,0:T(2,128)(2,1)S(1)} %get-tuple-element.60, bf16[1,16384]{1,0:T(2,128)(2,1)S(1)} %get-tuple-element.63, bf16[1,16384]{1,0:T(2,128)(2,1)} %get-tuple-element.85, bf16[1,16384]{1,0:T(2,128)(2,1)} %get-tuple-element.89, ...), dimensions={0} | concatenate | bytes 3145728 | tf_op jit(solution)/shard_map/stack | solution.py:267
  36.0 2.9 %stack.37.rk_ref = bf16[16,16384]{1,0:T(8,128)(2,1)S(1)} concatenate(bf16[1,16384]{1,0:T(2,128)(2,1)} %get-tuple-element.69, bf16[1,16384]{1,0:T(2,128)(2,1)} %get-tuple-element.61, bf16[1,16384]{1,0:T(2,128)(2,1)} %get-tuple-element.65, bf16[1,16384]{1,0:T(2,128)(2,1)} %get-tuple-element.86, bf16[1,16384]{1,0:T(2,128)(2,1)} %get-tuple-element.90, ...), dimensions={0} | concatenate | bytes 1048576 | tf_op jit(solution)/shard_map/stack | solution.py:266
  39.0 1.9 %fusion.5 = (bf16[16384,1]{0,1:T(2,128)(2,1)}, bf16[16384,1]{0,1:T(2,128)(2,1)S(1)}, bf16[16384,1]{0,1:T(2,128)(2,1)S(1)}, bf16[16384,1]{0,1:T(2,128)(2,1)}, bf1...) fusion(f32[16384,1]{0,1:T(1,128)} %bitcast.27, f32[16384,1]{0,1:T(1,128)} %bitcast.28), kind=kLoop, calls=%fused_computation.81 | loop fusion | flops 262144 | bytes 327680 | tf_op jit(solution)/shard_map/convert_element_type | solution.py:275
  40.8 1.9 %fusion.1 = (bf16[16384,1]{0,1:T(2,128)(2,1)}, bf16[16384,1]{0,1:T(2,128)(2,1)S(1)}, bf16[16384,1]{0,1:T(2,128)(2,1)S(1)}, bf16[16384,1]{0,1:T(2,128)(2,1)S(1)},...) fusion(f32[16384,1]{0,1:T(1,128)} %bitcast.25, f32[16384,1]{0,1:T(1,128)} %bitcast.26), kind=kLoop, calls=%fused_computation.77 | loop fusion | flops 262144 | bytes 327680 | tf_op jit(solution)/shard_map/convert_element_type | solution.py:275
  42.7 0.7 stack.32
  43.3 0.0 copy-start
  43.3 0.7 stack.33
  44.0 0.7 stack.34
  44.6 6.4 %stack.35 = bf16[16384,32]{0,1:T(8,128)(2,1)S(1)} concatenate(bf16[16384,1]{0,1:T(2,128)(2,1)S(1)} %get-tuple-element.106, bf16[16384,1]{0,1:T(2,128)(2,1)S(1)} %get-tuple-element.105, bf16[16384,1]{0,1:T(2,128)(2,1)S(1)} %get-tuple-element.106, bf16[16384,1]{0,1:T(2,128)(2,1)S(1)} %get-tuple-element.105, bf16[16384,1]{0,1:T(2,128)(2,1)} %get-tuple-element.104, ...), dimensions={1} | concatenate | bytes 2097152 | tf_op jit(solution)/shard_map/stack | solution.py:259
  51.0 3.1 %copy.18.s_ref = bf16[16384,32]{1,0:T(8,128)(2,1)} copy(bf16[16384,32]{0,1:T(8,128)(2,1)S(1)} %stack.35) | data formatting | bytes 2097152 | tf_op jit(solution)/shard_map/stack | solution.py:259
  54.1 0.0 copy-done
  54.1 0.0 copy-start.5
  54.2 0.0 copy-start.1
  54.2 0.0 copy-start.2
  54.2 0.0 copy-start.3
  54.2 0.1 fusion.75
  54.3 0.4 stack.31.t_ref
  54.8 83.9 %shard_map.96 = (f32[16,2048]{1,0:T(8,128)S(1)}, f32[48,2048]{1,0:T(8,128)S(1)}) custom-call(bf16[32,2048]{1,0:T(8,128)(2,1)S(1)} %stack.31.t_ref, bf16[16384,32]{1,0:T(8,128)(2,1)} %copy.18.s_ref, bf16[16,16384]{1,0:T(8,128)(2,1)S(1)} %stack.37.rk_ref, bf16[48,16384]{1,0:T(8,128)(2,1)S(1)} %stack.38.rg_ref), custom_call_target="tpu_custom_call" | custom-call | tf_op jit(solution)/shard_map/pallas_call | solution.py:116
  138.6 0.0 copy-done.5
  138.7 0.0 copy-done.4
  138.7 0.0 copy-done.6
  138.7 0.0 copy-done.1
  138.7 0.0 copy-done.2
  138.7 0.0 copy-done.3
  138.8 13.7 %shard_map.97 = (f32[3,2048]{1,0:T(4,128)S(1)}, f32[16,4,128]{2,1,0:T(4,128)S(1)}) custom-call(f32[16,2048]{1,0:T(8,128)S(1)} %get-tuple-element.4.ok_ref, f32[48,2048]{1,0:T(8,128)S(1)} %get-tuple-element.5.og_ref, f32[3,2048]{1,0:T(4,128)S(1)} %copy-done, f32[3,2048]{1,0:T(4,128)S(1)} %copy-done.1, f32[1,2048]{1,0:T(1,128)S(1)} %bitcast.15, ...), custom_call_target="tpu_custom_call" | custom-call | tf_op jit(solution)/shard_map/pallas_call | solution.py:230
  152.5 0.6 copy.21
  153.1 0.6 copy.22
  (10 shorter events, 0.1 us)
Async XLA Ops:
  43.3 10.8 %copy-start = (f32[3,2048]{1,0:T(4,128)S(1)}, f32[3,2048]{1,0:T(4,128)}, u32[]{:S(2)}) copy-start(f32[3,2048]{1,0:T(4,128)} %pos_ref.1) | copy-start | bytes 73732
  54.1 84.5 %copy-start.5 = (s32[2048,1]{0,1:T(1,128)S(1)}, s32[2048,1]{0,1:T(1,128)}, u32[]{:S(2)}) copy-start(s32[2048,1]{0,1:T(1,128)} %param.15) | copy-start | bytes 24580
  54.1 84.5 %copy-start.4 = (s32[2048]{0:T(1024)S(1)}, s32[2048]{0:T(1024)}, u32[]{:S(2)}) copy-start(s32[2048]{0:T(1024)} %param.14) | copy-start | bytes 24580
  54.1 84.5 %copy-start.6 = (s32[2048]{0:T(1024)S(1)}, s32[2048]{0:T(1024)}, u32[]{:S(2)}) copy-start(s32[2048]{0:T(1024)} %param.13) | copy-start | bytes 24580
  54.2 84.6 %copy-start.1 = (f32[3,2048]{1,0:T(4,128)S(1)}, f32[3,2048]{1,0:T(4,128)}, u32[]{:S(2)}) copy-start(f32[3,2048]{1,0:T(4,128)} %str_ref.1) | copy-start | bytes 73732
  54.2 84.6 %copy-start.2 = (f32[3,2048]{1,0:T(4,128)S(1)}, f32[3,2048]{1,0:T(4,128)}, u32[]{:S(2)}) copy-start(f32[3,2048]{1,0:T(4,128)} %frac_ref.1) | copy-start | bytes 73732
  54.2 84.6 %copy-start.3 = (f32[2048]{0:T(1024)S(1)}, f32[2048]{0:T(1024)}, u32[]{:S(2)}) copy-start(f32[2048]{0:T(1024)} %param.11) | copy-start | bytes 24580

commit v2 on v1

v2 whole, which is shorter than its diff:
```python
import functools
import math

import jax
import jax.numpy as jnp
from jax import lax
from jax.experimental import pallas as pl
from jax.experimental.pallas import tpu as pltpu
from jax.sharding import PartitionSpec as P

MESH = pl.DeviceIdType.MESH
f32, bf16 = jnp.float32, jnp.bfloat16
kernel_scale = 1.0 / (4.0 * math.pi)


def cross_rows(u, v):
    return [u[1] * v[2] - u[2] * v[1], u[2] * v[0] - u[0] * v[2], u[0] * v[1] - u[1] * v[0]]


def split(value, parts):
    pieces = []
    for _ in range(parts):
        piece = value.astype(bf16)
        pieces.append(piece)
        value = value - piece.astype(f32)
    return pieces


def spline_weight(distance):
    return jnp.where(
        distance < 1.0,
        1.0 - 2.5 * distance * distance + 1.5 * distance * distance * distance,
        0.5 * (2.0 - distance) * (2.0 - distance) * (1.0 - distance),
    )


def axis_weights(base, fraction, cells):
    local = fraction.shape[1]
    nodes = [
        spline_weight(fraction + 1.0),
        spline_weight(fraction),
        spline_weight(1.0 - fraction),
        spline_weight(2.0 - fraction),
    ]
    ids = lax.broadcasted_iota(jnp.int32, (cells, local), 0)
    total = jnp.zeros((cells, local), f32)
    for node in range(4):
        total = total + jnp.where(((base + (node - 1)) & (cells - 1)) == ids, nodes[node], 0.0)
    return total


TT, ST, CH = 256, 512, 64


def stack_split(value, parts):
    return [piece.astype(f32) for piece in split(value, parts)]


def step_kernel(
    n_dom, n_blk, pos_ref, str_ref, rad_ref, dye_ref, frac_ref, cell_ref, tile_ref, owner_ref,
    vel_ref, grid_ref,
    blocks_ref, tgt_ref, src_ref, rk_ref, rg_ref, ok_ref, og_ref, vk0, vk1, vg0, vg1, part_ref, got_ref,
    blk_send, blk_recv, dom_send, dom_recv,
):
    local = pos_ref.shape[1]
    dom, blk = lax.axis_index("dom"), lax.axis_index("blk")
    barrier = pltpu.get_barrier_semaphore()
    for step in range(1, n_blk):
        pl.semaphore_signal(barrier, inc=1, device_id={"blk": lax.rem(blk + step, n_blk)}, device_id_type=MESH)
    for step in range(1, n_dom):
        pl.semaphore_signal(barrier, inc=1, device_id={"dom": lax.rem(dom + step, n_dom)}, device_id_type=MESH)

    points = [pos_ref[i : i + 1, :] for i in range(3)]
    vortex = [str_ref[i : i + 1, :] for i in range(3)]
    radius = rad_ref[...]
    norm = points[0] * points[0] + points[1] * points[1] + points[2] * points[2]
    one, zero = jnp.ones_like(norm), jnp.zeros_like(norm)
    lead = [kernel_scale * row for row in vortex + cross_rows(vortex, points)]
    blocks_ref[0, 0:8, :] = jnp.concatenate(lead + [zero] * 2, 0)
    blocks_ref[0, 8:16, :] = jnp.concatenate(
        [-2.0 * row for row in points] + [norm + radius * radius, one] + [zero] * 3, 0
    )
    pl.semaphore_wait(barrier, n_blk - 1 + n_dom - 1)

    steps = list(range(2, n_blk, 2)) + list(range(1, n_blk, 2))
    blk_copies = []
    for slot, step in enumerate(steps, 1):
        copy = pltpu.make_async_remote_copy(
            src_ref=blocks_ref.at[0],
            dst_ref=blocks_ref.at[slot],
            send_sem=blk_send.at[slot],
            recv_sem=blk_recv.at[slot],
            device_id={"blk": lax.rem(blk + step, n_blk)},
            device_id_type=MESH,
        )
        copy.start()
        blk_copies.append(copy)

    t1, t2, t3 = stack_split(jnp.concatenate(points + [one, norm] + [zero] * 3, 0), 3)
    tgt_ref[...] = jnp.concatenate([t1, t2, t3, t1, t2, t1], 0).astype(bf16)
    ok_ref[...] = jnp.zeros_like(ok_ref)
    og_ref[...] = jnp.zeros_like(og_ref)

    vk, vg = (vk0, vk1), (vg0, vg1)
    chunks = local // ST
    count = chunks * (local // TT)

    def values(index, slot):
        start = pl.multiple_of(lax.rem(index, chunks) * ST, ST)
        targets = tgt_ref[:, pl.ds(pl.multiple_of(index // chunks * TT, TT), TT)]
        for row in range(0, ST, CH):
            square = jnp.dot(
                src_ref[pl.ds(pl.multiple_of(start + row, CH), CH), :], targets, preferred_element_type=f32
            )
            inverse = lax.rsqrt(square)
            second = inverse * inverse
            kern = second * inverse
            slope = kern * second
            kern_hi = kern.astype(bf16)
            slope_hi = slope.astype(bf16)
            vk[slot][row : row + CH, :] = kern_hi
            vg[slot][row : row + CH, :] = slope_hi
            vk[slot][ST + row : ST + row + CH, :] = (kern - kern_hi.astype(f32)).astype(bf16)
            vg[slot][ST + row : ST + row + CH, :] = (slope - slope_hi.astype(f32)).astype(bf16)

    def sums(index, slot):
        start = pl.multiple_of(lax.rem(index, chunks) * ST, ST)
        at = pl.multiple_of(index // chunks * TT, TT)
        rk = rk_ref[:, pl.ds(start, ST)]
        rg = rg_ref[:, pl.ds(start, ST)]
        ok_ref[:, pl.ds(at, TT)] += jnp.dot(
            jnp.concatenate([rk, rk], 1), vk[slot][...], preferred_element_type=f32
        )
        og_ref[:, pl.ds(at, TT)] += jnp.dot(
            jnp.concatenate([rg, rg], 1), vg[slot][...], preferred_element_type=f32
        )

    def block_tables(block):
        lead = blocks_ref[block, 0:8, :]
        place = blocks_ref[block, 8:16, :]
        hi, lo = split(lead, 2)
        rk_ref[0:8, :] = hi
        rk_ref[8:16, :] = lo
        for k in range(4):
            rows = lead if k == 0 else place[k - 1 : k, :] * lead
            hi, lo = split(rows, 2)
            rg_ref[8 * k : 8 * k + 8, :] = hi
            rg_ref[32 + 8 * k : 40 + 8 * k, :] = lo
        for at in range(0, local, 128):
            s1, s2, s3 = stack_split(place[:, at : at + 128], 3)
            src_ref[at : at + 128, :] = jnp.concatenate([s1, s1, s1, s2, s2, s3], 0).T.astype(bf16)

    @pl.loop(0, n_blk)
    def _(block):
        @pl.when(block > 0)
        def _():
            pltpu.make_async_remote_copy(
                src_ref=blocks_ref.at[0],
                dst_ref=blocks_ref.at[block],
                send_sem=blk_send.at[block],
                recv_sem=blk_recv.at[block],
                device_id={"blk": lax.rem(blk + 1, n_blk)},
                device_id_type=MESH,
            ).wait_recv()

        block_tables(block)
        values(0, 0)

        @pl.loop(0, count // 2)
        def _(pair):
            values(2 * pair + 1, 1)
            sums(2 * pair, 0)
            values(jnp.minimum(2 * pair + 2, count - 1), 0)
            sums(2 * pair + 1, 1)

    for copy in blk_copies:
        copy.wait_send()

    first = ok_ref[0:8, :] + ok_ref[8:16, :]
    first = [first[i : i + 1, :] for i in range(6)]
    second = []
    for k in range(4):
        rows = og_ref[8 * k : 8 * k + 8, :] + og_ref[32 + 8 * k : 40 + 8 * k, :]
        second.append([rows[i : i + 1, :] for i in range(6)])
    turned = cross_rows(first[0:3], points)
    velocity = [turned[i] - first[3 + i] for i in range(3)]
    for i in range(3):
        vel_ref[i : i + 1, :] = velocity[i]
    term_one = cross_rows(first[0:3], vortex)
    dot_self = vortex[0] * points[0] + vortex[1] * points[1] + vortex[2] * points[2]
    mixed_one = [-0.5 * sum(vortex[k] * second[1 + k][i] for k in range(3)) for i in range(3)]
    mixed_two = [-0.5 * sum(vortex[k] * second[1 + k][3 + i] for k in range(3)) for i in range(3)]
    slope_turned = cross_rows(second[0][0:3], points)
    mixed_turned = cross_rows(mixed_one, points)
    carried = []
    for i in range(3):
        term_two = dot_self * (slope_turned[i] - second[0][3 + i]) - mixed_turned[i] + mixed_two[i]
        carried.append((vortex[i] + 0.02 * (term_one[i] - 3.0 * term_two)) * 32.0)
    carried.append(dye_ref[...] * 32.0)

    cell = cell_ref[...]
    starts = [cell & 7, (cell >> 3) & 3, cell >> 5]
    weights = []
    for i in range(3):
        coords = starts[i].astype(f32) + frac_ref[i : i + 1, :] + 2.0 * velocity[i]
        lowest = jnp.floor(coords)
        weights.append(axis_weights(lowest.astype(jnp.int32), coords - lowest, 8 if i == 0 else 4))
    plane = [weights[2][z : z + 1, :] * weights[1][y : y + 1, :] for z in range(4) for y in range(4)]

    tiles = grid_ref.shape[0]
    tile = owner_ref[...] * tiles + tile_ref[...]
    ids = lax.broadcasted_iota(jnp.int32, (n_dom * tiles, local), 0)
    onehot = jnp.where(ids == tile, 1.0, 0.0).astype(bf16)
    for c in range(4):
        spread = jnp.concatenate([weights[0] * (plane[k] * carried[c]) for k in range(16)], 0)
        total = jnp.zeros((n_dom * tiles, 128), f32)
        for piece in split(spread, 2):
            total = total + lax.dot_general(
                onehot, piece, (((1,), (1,)), ((), ())), preferred_element_type=f32
            )
        part_ref[:, :, c, :] = total.reshape(n_dom, tiles, 128)

    dom_copies = []
    for step in range(1, n_dom):
        peer = lax.rem(dom + step, n_dom)
        copy = pltpu.make_async_remote_copy(
            src_ref=part_ref.at[peer],
            dst_ref=got_ref.at[step],
            send_sem=dom_send.at[step],
            recv_sem=dom_recv.at[step],
            device_id={"dom": peer},
            device_id_type=MESH,
        )
        copy.start()
        dom_copies.append(copy)
    total = part_ref[dom]
    for step in range(1, n_dom):
        dom_copies[step - 1].wait_recv()
        total = total + got_ref[step]
    grid_ref[...] = total
    for copy in dom_copies:
        copy.wait_send()


def on_device(
    positions, strength, core_radius, dye_amount, cell_fraction, cell_index, tile_local, owner_dom
):
    n_dom, n_blk = lax.axis_size("dom"), lax.axis_size("blk")
    local = positions.shape[1]
    tiles = local // 128
    vmem = pl.BlockSpec(memory_space=pltpu.VMEM)
    return pl.pallas_call(
        functools.partial(step_kernel, n_dom, n_blk),
        out_shape=(
            jax.ShapeDtypeStruct((3, local), f32),
            jax.ShapeDtypeStruct((tiles, 4, 128), f32),
        ),
        in_specs=[vmem] * 8,
        out_specs=(vmem, vmem),
        scratch_shapes=[
            pltpu.VMEM((n_blk, 16, local), f32),
            pltpu.VMEM((48, local), bf16),
            pltpu.VMEM((local, 48), bf16),
            pltpu.VMEM((16, local), bf16),
            pltpu.VMEM((64, local), bf16),
            pltpu.VMEM((16, local), f32),
            pltpu.VMEM((64, local), f32),
        ]
        + [pltpu.VMEM((2 * ST, TT), bf16)] * 4
        + [pltpu.VMEM((n_dom, tiles, 4, 128), f32)] * 2
        + [pltpu.SemaphoreType.DMA((n_blk,))] * 2
        + [pltpu.SemaphoreType.DMA((n_dom,))] * 2,
        compiler_params=pltpu.CompilerParams(collective_id=0, has_side_effects=True, vmem_limit_bytes=56 << 20),
    )(
        positions, strength, core_radius[None], dye_amount[None], cell_fraction, cell_index[None],
        tile_local[None], owner_dom.reshape(1, local),
    )


def solution(mesh):
    both = ("dom", "blk")
    placed = (P(None, both), P(None, both), P(both), P(both), P(None, both), P(both), P(both), P(both, None))
    return jax.shard_map(
        on_device,
        mesh=mesh,
        in_specs=placed,
        out_specs=(P(None, both), P(both, None, None)),
        check_vma=False,
    )
```

time: 156 us -> 109 us (0.70); the launches traced: 154 us -> 108 us
  local copies, waits for them, and re-layouts: 25.6 us -> 2 us
  other arithmetic: 15.4 us -> 0 us
  Pallas kernels: 112 us -> 106 us
    another operation x12 -> x0, local copies, waits for them, and re-layouts: 24.4 us -> none  [the longest x5 11.5 us: source_tables(): sources = jnp.stack(rows, axis=1)]
    convert_element_type x6 -> x0, other arithmetic: 10.2 us -> none  [split_whole(): pieces.append(piece.astype(bf16))]
    pallas_call x3 -> x1, Pallas kernels: 112 us -> 106 us  [on_device(): pl.pallas_call(functools.partial(step_kernel, n_dom, n_blk), out_shape=(j...]
    slice x1 -> x0, other arithmetic: 3.72 us -> none  [source_tables(): points = [blocks[:, i].reshape(-1) for i in range(3)]]
where the time goes in v2:
time: 109 us; the launch traced here: 108 us
  Pallas kernels  106 us (97%)
  local copies, waits for them, and re-layouts  2 us (2%)
    pallas_call x1, Pallas kernels, on_device(): pl.pallas_call(functools.partial(step_kernel, n_dom, n_blk), out_shape=(j...  106 us

profile of v2, /device:TPU:25, one launch (start us, length us, event | category | flops | bytes accessed | tf_op | source)
XLA Modules:
  0.0 108.3 jit_solution(13669664041807845621)
XLA Ops:
  0.6 105.6 %shard_map.95 = (f32[3,2048]{1,0:T(4,128)}, f32[16,4,128]{2,1,0:T(4,128)}) custom-call(f32[3,2048]{1,0:T(4,128)} %pos_ref.1, f32[3,2048]{1,0:T(4,128)} %str_ref.1, f32[1,2048]{1,0:T(1,128)} %bitcast.5, f32[1,2048]{1,0:T(1,128)} %bitcast.6, f32[3,2048]{1,0:T(4,128)} %frac_ref.1, s32[1,2048]{1,0:T(1,128)} %bitcast.7, s32[1,2048]{1,0:T(1,128)} %bitcast.8, ...), custom_call_target="tpu_custom_call" | custom-call | tf_op jit(solution)/shard_map/pallas_call | solution.py:252
  106.3 0.0 copy-start
  106.3 1.4 %copy.12 = f32[3,2048]{1,0:T(4,128)} copy(f32[3,2048]{1,0:T(4,128)} %get-tuple-element.4) | data formatting | bytes 49152
  107.7 0.0 copy-done
  107.7 0.6 copy.13
Async XLA Ops:
  106.3 1.4 %copy-start = (f32[16,4,128]{2,1,0:T(4,128)S(1)}, f32[16,4,128]{2,1,0:T(4,128)}, u32[]{:S(2)}) copy-start(f32[16,4,128]{2,1,0:T(4,128)} %get-tuple-element.5) | copy-start | bytes 98308

commit v3 on v2

--- a/solution.py
+++ b/solution.py
@@ -49,7 +49,7 @@
     return total
 
 
-TT, ST, CH = 256, 512, 64
+TT, ST, UNROLL = 256, 512, 16
 
 
 def stack_split(value, parts):
@@ -59,7 +59,7 @@
 def step_kernel(
     n_dom, n_blk, pos_ref, str_ref, rad_ref, dye_ref, frac_ref, cell_ref, tile_ref, owner_ref,
     vel_ref, grid_ref,
-    blocks_ref, tgt_ref, src_ref, rk_ref, rg_ref, ok_ref, og_ref, vk0, vk1, vg0, vg1, part_ref, got_ref,
+    blocks_ref, tgt_ref, src_ref, rk_ref, rg_ref, ok_ref, og_ref, q0, q1, vk0, vk1, vg0, vg1, part_ref, got_ref,
     blk_send, blk_recv, dom_send, dom_recv,
 ):
     local = pos_ref.shape[1]
@@ -101,33 +101,41 @@
     ok_ref[...] = jnp.zeros_like(ok_ref)
     og_ref[...] = jnp.zeros_like(og_ref)
 
-    vk, vg = (vk0, vk1), (vg0, vg1)
+    qs, vk, vg = (q0, q1), (vk0, vk1), (vg0, vg1)
     chunks = local // ST
     count = chunks * (local // TT)
-
-    def values(index, slot):
-        start = pl.multiple_of(lax.rem(index, chunks) * ST, ST)
-        targets = tgt_ref[:, pl.ds(pl.multiple_of(index // chunks * TT, TT), TT)]
-        for row in range(0, ST, CH):
-            square = jnp.dot(
-                src_ref[pl.ds(pl.multiple_of(start + row, CH), CH), :], targets, preferred_element_type=f32
-            )
-            inverse = lax.rsqrt(square)
-            second = inverse * inverse
-            kern = second * inverse
-            slope = kern * second
-            kern_hi = kern.astype(bf16)
-            slope_hi = slope.astype(bf16)
-            vk[slot][row : row + CH, :] = kern_hi
-            vg[slot][row : row + CH, :] = slope_hi
-            vk[slot][ST + row : ST + row + CH, :] = (kern - kern_hi.astype(f32)).astype(bf16)
-            vg[slot][ST + row : ST + row + CH, :] = (slope - slope_hi.astype(f32)).astype(bf16)
+    halves = count // UNROLL
+
+    def place_of(index):
+        step = lax.rem(index, count)
+        return (
+            lax.rem(index // count, 2),
+            pl.multiple_of(lax.rem(step, chunks) * ST, ST),
+            pl.multiple_of(step // chunks * TT, TT),
+        )
+
+    def squares(index, slot):
+        side, start, at = place_of(index)
+        qs[slot][...] = jnp.dot(
+            src_ref[side, pl.ds(start, ST), :], tgt_ref[:, pl.ds(at, TT)], preferred_element_type=f32
+        )
+
+    def values(slot):
+        inverse = lax.rsqrt(qs[slot][...])
+        second = inverse * inverse
+        kern = second * inverse
+        slope = kern * second
+        kern_hi = kern.astype(bf16)
+        slope_hi = slope.astype(bf16)
+        vk[slot][0:ST, :] = kern_hi
+        vg[slot][0:ST, :] = slope_hi
+        vk[slot][ST:, :] = (kern - kern_hi.astype(f32)).astype(bf16)
+        vg[slot][ST:, :] = (slope - slope_hi.astype(f32)).astype(bf16)
 
     def sums(index, slot):
-        start = pl.multiple_of(lax.rem(index, chunks) * ST, ST)
-        at = pl.multiple_of(index // chunks * TT, TT)
-        rk = rk_ref[:, pl.ds(start, ST)]
-        rg = rg_ref[:, pl.ds(start, ST)]
+        side, start, at = place_of(index)
+        rk = rk_ref[side, :, pl.ds(start, ST)]
+        rg = rg_ref[side, :, pl.ds(start, ST)]
         ok_ref[:, pl.ds(at, TT)] += jnp.dot(
             jnp.concatenate([rk, rk], 1), vk[slot][...], preferred_element_type=f32
         )
@@ -136,23 +144,31 @@
         )
 
     def block_tables(block):
+        side = lax.rem(block, 2)
         lead = blocks_ref[block, 0:8, :]
         place = blocks_ref[block, 8:16, :]
         hi, lo = split(lead, 2)
-        rk_ref[0:8, :] = hi
-        rk_ref[8:16, :] = lo
+        rk_ref[side, 0:8, :] = hi
+        rk_ref[side, 8:16, :] = lo
         for k in range(4):
             rows = lead if k == 0 else place[k - 1 : k, :] * lead
             hi, lo = split(rows, 2)
-            rg_ref[8 * k : 8 * k + 8, :] = hi
-            rg_ref[32 + 8 * k : 40 + 8 * k, :] = lo
+            rg_ref[side, 8 * k : 8 * k + 8, :] = hi
+            rg_ref[side, 32 + 8 * k : 40 + 8 * k, :] = lo
         for at in range(0, local, 128):
             s1, s2, s3 = stack_split(place[:, at : at + 128], 3)
-            src_ref[at : at + 128, :] = jnp.concatenate([s1, s1, s1, s2, s2, s3], 0).T.astype(bf16)
-
-    @pl.loop(0, n_blk)
-    def _(block):
-        @pl.when(block > 0)
+            src_ref[side, at : at + 128, :] = jnp.concatenate([s1, s1, s1, s2, s2, s3], 0).T.astype(bf16)
+
+    block_tables(0)
+    squares(0, 0)
+    values(0)
+    squares(1, 1)
+
+    @pl.loop(0, n_blk * halves)
+    def _(part):
+        block = part // halves + 1
+
+        @pl.when((lax.rem(part, halves) == halves - 1) & (block < n_blk))
         def _():
             pltpu.make_async_remote_copy(
                 src_ref=blocks_ref.at[0],
@@ -162,16 +178,14 @@
                 device_id={"blk": lax.rem(blk + 1, n_blk)},
                 device_id_type=MESH,
             ).wait_recv()
-
-        block_tables(block)
-        values(0, 0)
-
-        @pl.loop(0, count // 2)
-        def _(pair):
-            values(2 * pair + 1, 1)
-            sums(2 * pair, 0)
-            values(jnp.minimum(2 * pair + 2, count - 1), 0)
-            sums(2 * pair + 1, 1)
+            block_tables(block)
+
+        for step in range(UNROLL):
+            index = UNROLL * part + step
+            slot = step % 2
+            sums(index, slot)
+            values(1 - slot)
+            squares(jnp.minimum(index + 2, n_blk * count - 1), slot)
 
     for copy in blk_copies:
         copy.wait_send()
@@ -260,12 +274,13 @@
         scratch_shapes=[
             pltpu.VMEM((n_blk, 16, local), f32),
             pltpu.VMEM((48, local), bf16),
-            pltpu.VMEM((local, 48), bf16),
-            pltpu.VMEM((16, local), bf16),
-            pltpu.VMEM((64, local), bf16),
+            pltpu.VMEM((2, local, 48), bf16),
+            pltpu.VMEM((2, 16, local), bf16),
+            pltpu.VMEM((2, 64, local), bf16),
             pltpu.VMEM((16, local), f32),
             pltpu.VMEM((64, local), f32),
         ]
+        + [pltpu.VMEM((ST, TT), f32)] * 2
         + [pltpu.VMEM((2 * ST, TT), bf16)] * 4
         + [pltpu.VMEM((n_dom, tiles, 4, 128), f32)] * 2
         + [pltpu.SemaphoreType.DMA((n_blk,))] * 2

time: 109 us -> 95.5 us (0.88)
  Pallas kernels: 106 us -> 92.6 us
    pallas_call x1, Pallas kernels: 106 us -> 92.6 us  [on_device(): pl.pallas_call(functools.partial(step_kernel, n_dom, n_blk), out_shape=(j...]
where the time goes in v3:
time: 95.5 us; the launch traced here: 95.3 us
  Pallas kernels  92.6 us (97%)
  local copies, waits for them, and re-layouts  2 us (2%)
    pallas_call x1, Pallas kernels, on_device(): pl.pallas_call(functools.partial(step_kernel, n_dom, n_blk), out_shape=(j...  92.6 us
    unnamed x4, local copies, waits for them, and re-layouts  2 us

profile of v3, /device:TPU:25, one launch (start us, length us, event | category | flops | bytes accessed | tf_op | source)
XLA Modules:
  0.0 95.3 jit_solution(12476841804671181419)
XLA Ops:
  0.6 92.6 %shard_map.95 = (f32[3,2048]{1,0:T(4,128)}, f32[16,4,128]{2,1,0:T(4,128)}) custom-call(f32[3,2048]{1,0:T(4,128)} %pos_ref.1, f32[3,2048]{1,0:T(4,128)} %str_ref.1, f32[1,2048]{1,0:T(1,128)} %bitcast.5, f32[1,2048]{1,0:T(1,128)} %bitcast.6, f32[3,2048]{1,0:T(4,128)} %frac_ref.1, s32[1,2048]{1,0:T(1,128)} %bitcast.7, s32[1,2048]{1,0:T(1,128)} %bitcast.8, ...), custom_call_target="tpu_custom_call" | custom-call | tf_op jit(solution)/shard_map/pallas_call | solution.py:266
  93.3 0.0 copy-start
  93.3 1.4 %copy.12 = f32[3,2048]{1,0:T(4,128)} copy(f32[3,2048]{1,0:T(4,128)} %get-tuple-element.4) | data formatting | bytes 49152
  94.7 0.0 copy-done
  94.7 0.6 copy.13
Async XLA Ops:
  93.3 1.4 %copy-start = (f32[16,4,128]{2,1,0:T(4,128)S(1)}, f32[16,4,128]{2,1,0:T(4,128)}, u32[]{:S(2)}) copy-start(f32[16,4,128]{2,1,0:T(4,128)} %get-tuple-element.5) | copy-start | bytes 98308

commit v4 on v3

--- a/solution.py
+++ b/solution.py
@@ -49,7 +49,7 @@
     return total
 
 
-TT, ST, UNROLL = 256, 512, 16
+TT, ST, PIECE, CHUNK, UNROLL = 256, 512, 128, 32, 16
 
 
 def stack_split(value, parts):
@@ -59,7 +59,7 @@
 def step_kernel(
     n_dom, n_blk, pos_ref, str_ref, rad_ref, dye_ref, frac_ref, cell_ref, tile_ref, owner_ref,
     vel_ref, grid_ref,
-    blocks_ref, tgt_ref, src_ref, rk_ref, rg_ref, ok_ref, og_ref, q0, q1, vk0, vk1, vg0, vg1, part_ref, got_ref,
+    blocks_ref, tgt_ref, src_ref, rk_ref, rg_ref, ok_ref, og_ref, q0, q1, part_ref, got_ref,
     blk_send, blk_recv, dom_send, dom_recv,
 ):
     local = pos_ref.shape[1]
@@ -101,7 +101,7 @@
     ok_ref[...] = jnp.zeros_like(ok_ref)
     og_ref[...] = jnp.zeros_like(og_ref)
 
-    qs, vk, vg = (q0, q1), (vk0, vk1), (vg0, vg1)
+    qs = (q0, q1)
     chunks = local // ST
     count = chunks * (local // TT)
     halves = count // UNROLL
@@ -114,55 +114,65 @@
             pl.multiple_of(step // chunks * TT, TT),
         )
 
-    def squares(index, slot):
+    def squares(index, slot, row):
         side, start, at = place_of(index)
-        qs[slot][...] = jnp.dot(
-            src_ref[side, pl.ds(start, ST), :], tgt_ref[:, pl.ds(at, TT)], preferred_element_type=f32
-        )
-
-    def values(slot):
-        inverse = lax.rsqrt(qs[slot][...])
-        second = inverse * inverse
-        kern = second * inverse
-        slope = kern * second
-        kern_hi = kern.astype(bf16)
-        slope_hi = slope.astype(bf16)
-        vk[slot][0:ST, :] = kern_hi
-        vg[slot][0:ST, :] = slope_hi
-        vk[slot][ST:, :] = (kern - kern_hi.astype(f32)).astype(bf16)
-        vg[slot][ST:, :] = (slope - slope_hi.astype(f32)).astype(bf16)
-
-    def sums(index, slot):
+        qs[slot][row : row + PIECE, :] = jnp.dot(
+            src_ref[side, pl.ds(pl.multiple_of(start + row, PIECE), PIECE), :],
+            tgt_ref[:, pl.ds(at, TT)],
+            preferred_element_type=f32,
+        )
+
+    def values(slot, row, kern_parts, slope_parts):
+        for at in range(row, row + PIECE, CHUNK):
+            inverse = lax.rsqrt(qs[slot][at : at + CHUNK, :])
+            second = inverse * inverse
+            kern = second * inverse
+            slope = kern * second
+            kern_hi = kern.astype(bf16)
+            slope_hi = slope.astype(bf16)
+            kern_parts += [kern_hi, (kern - kern_hi.astype(f32)).astype(bf16)]
+            slope_parts += [slope_hi, (slope - slope_hi.astype(f32)).astype(bf16)]
+
+    def sums(index, kern_parts, slope_parts):
         side, start, at = place_of(index)
-        rk = rk_ref[side, :, pl.ds(start, ST)]
-        rg = rg_ref[side, :, pl.ds(start, ST)]
+        twice = pl.ds(pl.multiple_of(2 * start, 2 * ST), 2 * ST)
         ok_ref[:, pl.ds(at, TT)] += jnp.dot(
-            jnp.concatenate([rk, rk], 1), vk[slot][...], preferred_element_type=f32
+            rk_ref[side, :, twice], jnp.concatenate(kern_parts, 0), preferred_element_type=f32
         )
         og_ref[:, pl.ds(at, TT)] += jnp.dot(
-            jnp.concatenate([rg, rg], 1), vg[slot][...], preferred_element_type=f32
-        )
+            rg_ref[side, :, twice], jnp.concatenate(slope_parts, 0), preferred_element_type=f32
+        )
+
+    column = lax.broadcasted_iota(jnp.int32, (128, 256), 1)
+    origin = (column // (2 * CHUNK)) * CHUNK + column % CHUNK
+    double = jnp.where(lax.broadcasted_iota(jnp.int32, (128, 256), 0) == origin, 1.0, 0.0).astype(bf16)
 
     def block_tables(block):
         side = lax.rem(block, 2)
         lead = blocks_ref[block, 0:8, :]
         place = blocks_ref[block, 8:16, :]
-        hi, lo = split(lead, 2)
-        rk_ref[side, 0:8, :] = hi
-        rk_ref[side, 8:16, :] = lo
-        for k in range(4):
-            rows = lead if k == 0 else place[k - 1 : k, :] * lead
-            hi, lo = split(rows, 2)
-            rg_ref[side, 8 * k : 8 * k + 8, :] = hi
-            rg_ref[side, 32 + 8 * k : 40 + 8 * k, :] = lo
+        groups = [split(lead if k == 0 else place[k - 1 : k, :] * lead, 2) for k in range(4)]
+        rows = jnp.concatenate(
+            [g.astype(f32) for g in groups[0]]
+            + [g[0].astype(f32) for g in groups]
+            + [g[1].astype(f32) for g in groups],
+            0,
+        ).astype(bf16)
+        doubled = jnp.dot(
+            jnp.concatenate([rows[:, at : at + 128] for at in range(0, local, 128)], 0),
+            double,
+            preferred_element_type=f32,
+        ).astype(bf16)
+        for k in range(local // 128):
+            rk_ref[side, :, 256 * k : 256 * k + 256] = doubled[80 * k : 80 * k + 16]
+            rg_ref[side, :, 256 * k : 256 * k + 256] = doubled[80 * k + 16 : 80 * k + 80]
         for at in range(0, local, 128):
             s1, s2, s3 = stack_split(place[:, at : at + 128], 3)
             src_ref[side, at : at + 128, :] = jnp.concatenate([s1, s1, s1, s2, s2, s3], 0).T.astype(bf16)
 
     block_tables(0)
-    squares(0, 0)
-    values(0)
-    squares(1, 1)
+    for row in range(0, ST, PIECE):
+        squares(0, 0, row)
 
     @pl.loop(0, n_blk * halves)
     def _(part):
@@ -183,9 +193,11 @@
         for step in range(UNROLL):
             index = UNROLL * part + step
             slot = step % 2
-            sums(index, slot)
-            values(1 - slot)
-            squares(jnp.minimum(index + 2, n_blk * count - 1), slot)
+            kern_parts, slope_parts = [], []
+            for row in range(0, ST, PIECE):
+                squares(jnp.minimum(index + 1, n_blk * count - 1), 1 - slot, row)
+                values(slot, row, kern_parts, slope_parts)
+            sums(index, kern_parts, slope_parts)
 
     for copy in blk_copies:
         copy.wait_send()
@@ -225,33 +237,37 @@
     tile = owner_ref[...] * tiles + tile_ref[...]
     ids = lax.broadcasted_iota(jnp.int32, (n_dom * tiles, local), 0)
     onehot = jnp.where(ids == tile, 1.0, 0.0).astype(bf16)
-    for c in range(4):
-        spread = jnp.concatenate([weights[0] * (plane[k] * carried[c]) for k in range(16)], 0)
-        total = jnp.zeros((n_dom * tiles, 128), f32)
-        for piece in split(spread, 2):
-            total = total + lax.dot_general(
-                onehot, piece, (((1,), (1,)), ((), ())), preferred_element_type=f32
+    twice = jnp.concatenate([onehot, onehot], 1)
+    dom_copies = []
+    for pair in range(2):
+        spread = jnp.concatenate(
+            [weights[0] * (plane[k] * carried[2 * pair + c]) for c in range(2) for k in range(16)], 0
+        )
+        part_ref[pair] = lax.dot_general(
+            twice,
+            jnp.concatenate(split(spread, 2), 1),
+            (((1,), (1,)), ((), ())),
+            preferred_element_type=f32,
+        ).reshape(n_dom, tiles, 256)
+        for step in range(1, n_dom):
+            peer = lax.rem(dom + step, n_dom)
+            copy = pltpu.make_async_remote_copy(
+                src_ref=part_ref.at[pair, peer],
+                dst_ref=got_ref.at[pair, step],
+                send_sem=dom_send.at[pair, step],
+                recv_sem=dom_recv.at[pair, step],
+                device_id={"dom": peer},
+                device_id_type=MESH,
             )
-        part_ref[:, :, c, :] = total.reshape(n_dom, tiles, 128)
-
-    dom_copies = []
-    for step in range(1, n_dom):
-        peer = lax.rem(dom + step, n_dom)
-        copy = pltpu.make_async_remote_copy(
-            src_ref=part_ref.at[peer],
-            dst_ref=got_ref.at[step],
-            send_sem=dom_send.at[step],
-            recv_sem=dom_recv.at[step],
-            device_id={"dom": peer},
-            device_id_type=MESH,
-        )
-        copy.start()
-        dom_copies.append(copy)
-    total = part_ref[dom]
-    for step in range(1, n_dom):
-        dom_copies[step - 1].wait_recv()
-        total = total + got_ref[step]
-    grid_ref[...] = total
+            copy.start()
+            dom_copies.append(copy)
+    for pair in range(2):
+        total = part_ref[pair, dom]
+        for step in range(1, n_dom):
+            dom_copies[pair * (n_dom - 1) + step - 1].wait_recv()
+            total = total + got_ref[pair, step]
+        for c in range(2):
+            grid_ref[:, 2 * pair + c, :] = total[:, 128 * c : 128 * c + 128]
     for copy in dom_copies:
         copy.wait_send()
 
@@ -275,16 +291,15 @@
             pltpu.VMEM((n_blk, 16, local), f32),
             pltpu.VMEM((48, local), bf16),
             pltpu.VMEM((2, local, 48), bf16),
-            pltpu.VMEM((2, 16, local), bf16),
-            pltpu.VMEM((2, 64, local), bf16),
+            pltpu.VMEM((2, 16, 2 * local), bf16),
+            pltpu.VMEM((2, 64, 2 * local), bf16),
             pltpu.VMEM((16, local), f32),
             pltpu.VMEM((64, local), f32),
         ]
         + [pltpu.VMEM((ST, TT), f32)] * 2
-        + [pltpu.VMEM((2 * ST, TT), bf16)] * 4
-        + [pltpu.VMEM((n_dom, tiles, 4, 128), f32)] * 2
+        + [pltpu.VMEM((2, n_dom, tiles, 256), f32)] * 2
         + [pltpu.SemaphoreType.DMA((n_blk,))] * 2
-        + [pltpu.SemaphoreType.DMA((n_dom,))] * 2,
+        + [pltpu.SemaphoreType.DMA((2, n_dom))] * 2,
         compiler_params=pltpu.CompilerParams(collective_id=0, has_side_effects=True, vmem_limit_bytes=56 << 20),
     )(
         positions, strength, core_radius[None], dye_amount[None], cell_fraction, cell_index[None],

time: 95.5 us -> 90.5 us (0.948)
  Pallas kernels: 92.6 us -> 87.6 us
    pallas_call x1, Pallas kernels: 92.6 us -> 87.6 us  [on_device(): pl.pallas_call(functools.partial(step_kernel, n_dom, n_blk), out_shape=(j...]
where the time goes in v4:
time: 90.5 us; the launch traced here: 90.2 us
  Pallas kernels  87.6 us (97%)
  local copies, waits for them, and re-layouts  2 us (2%)
    pallas_call x1, Pallas kernels, on_device(): pl.pallas_call(functools.partial(step_kernel, n_dom, n_blk), out_shape=(j...  87.6 us
    unnamed x4, local copies, waits for them, and re-layouts  2 us

profile of v4, /device:TPU:25, one launch (start us, length us, event | category | flops | bytes accessed | tf_op | source)
XLA Modules:
  0.0 90.2 jit_solution(9140607550514743213)
XLA Ops:
  0.6 87.6 %shard_map.95 = (f32[3,2048]{1,0:T(4,128)}, f32[16,4,128]{2,1,0:T(4,128)}) custom-call(f32[3,2048]{1,0:T(4,128)} %pos_ref.1, f32[3,2048]{1,0:T(4,128)} %str_ref.1, f32[1,2048]{1,0:T(1,128)} %bitcast.5, f32[1,2048]{1,0:T(1,128)} %bitcast.6, f32[3,2048]{1,0:T(4,128)} %frac_ref.1, s32[1,2048]{1,0:T(1,128)} %bitcast.7, s32[1,2048]{1,0:T(1,128)} %bitcast.8, ...), custom_call_target="tpu_custom_call" | custom-call | tf_op jit(solution)/shard_map/pallas_call | solution.py:282
  88.2 0.0 copy-start
  88.2 1.4 %copy.12 = f32[3,2048]{1,0:T(4,128)} copy(f32[3,2048]{1,0:T(4,128)} %get-tuple-element.4) | data formatting | bytes 49152
  89.6 0.0 copy-done
  89.6 0.6 copy.13
Async XLA Ops:
  88.2 1.4 %copy-start = (f32[16,4,128]{2,1,0:T(4,128)S(1)}, f32[16,4,128]{2,1,0:T(4,128)}, u32[]{:S(2)}) copy-start(f32[16,4,128]{2,1,0:T(4,128)} %get-tuple-element.5) | copy-start | bytes 98308

commit v5 on v4

--- a/solution.py
+++ b/solution.py
@@ -26,22 +26,16 @@
     return pieces
 
 
-def spline_weight(distance):
-    return jnp.where(
-        distance < 1.0,
-        1.0 - 2.5 * distance * distance + 1.5 * distance * distance * distance,
-        0.5 * (2.0 - distance) * (2.0 - distance) * (1.0 - distance),
-    )
-
-
-def axis_weights(base, fraction, cells):
-    local = fraction.shape[1]
-    nodes = [
-        spline_weight(fraction + 1.0),
-        spline_weight(fraction),
-        spline_weight(1.0 - fraction),
-        spline_weight(2.0 - fraction),
-    ]
+def inner(u):
+    return 1.0 - 2.5 * u * u + 1.5 * u * u * u
+
+
+def outer(u):
+    return 0.5 * (2.0 - u) * (2.0 - u) * (1.0 - u)
+
+
+def axis_weights(base, nodes, cells):
+    local = base.shape[1]
     ids = lax.broadcasted_iota(jnp.int32, (cells, local), 0)
     total = jnp.zeros((cells, local), f32)
     for node in range(4):
@@ -59,16 +53,17 @@
 def step_kernel(
     n_dom, n_blk, pos_ref, str_ref, rad_ref, dye_ref, frac_ref, cell_ref, tile_ref, owner_ref,
     vel_ref, grid_ref,
-    blocks_ref, tgt_ref, src_ref, rk_ref, rg_ref, ok_ref, og_ref, q0, q1, part_ref, got_ref,
-    blk_send, blk_recv, dom_send, dom_recv,
+    blocks_ref, tgt_ref, src_ref, rk_ref, rg_ref, ok_ref, og_ref, q0, q1, part_ref, side_ref, both_ref, got_ref,
+    blk_send, blk_recv, dom_send, dom_recv, near_send, near_recv,
 ):
     local = pos_ref.shape[1]
     dom, blk = lax.axis_index("dom"), lax.axis_index("blk")
     barrier = pltpu.get_barrier_semaphore()
     for step in range(1, n_blk):
         pl.semaphore_signal(barrier, inc=1, device_id={"blk": lax.rem(blk + step, n_blk)}, device_id_type=MESH)
-    for step in range(1, n_dom):
+    for step in range(2, n_dom, 2):
         pl.semaphore_signal(barrier, inc=1, device_id={"dom": lax.rem(dom + step, n_dom)}, device_id_type=MESH)
+    pl.semaphore_signal(barrier, inc=1, device_id={"dom": dom + 1 - 2 * lax.rem(dom, 2)}, device_id_type=MESH)
 
     points = [pos_ref[i : i + 1, :] for i in range(3)]
     vortex = [str_ref[i : i + 1, :] for i in range(3)]
@@ -80,7 +75,7 @@
     blocks_ref[0, 8:16, :] = jnp.concatenate(
         [-2.0 * row for row in points] + [norm + radius * radius, one] + [zero] * 3, 0
     )
-    pl.semaphore_wait(barrier, n_blk - 1 + n_dom - 1)
+    pl.semaphore_wait(barrier, n_blk - 1 + n_dom // 2)
 
     steps = list(range(2, n_blk, 2)) + list(range(1, n_blk, 2))
     blk_copies = []
@@ -210,8 +205,7 @@
         second.append([rows[i : i + 1, :] for i in range(6)])
     turned = cross_rows(first[0:3], points)
     velocity = [turned[i] - first[3 + i] for i in range(3)]
-    for i in range(3):
-        vel_ref[i : i + 1, :] = velocity[i]
+    vel_ref[...] = jnp.concatenate(velocity, 0)
     term_one = cross_rows(first[0:3], vortex)
     dot_self = vortex[0] * points[0] + vortex[1] * points[1] + vortex[2] * points[2]
     mixed_one = [-0.5 * sum(vortex[k] * second[1 + k][i] for k in range(3)) for i in range(3)]
@@ -225,12 +219,16 @@
     carried.append(dye_ref[...] * 32.0)
 
     cell = cell_ref[...]
-    starts = [cell & 7, (cell >> 3) & 3, cell >> 5]
-    weights = []
-    for i in range(3):
-        coords = starts[i].astype(f32) + frac_ref[i : i + 1, :] + 2.0 * velocity[i]
-        lowest = jnp.floor(coords)
-        weights.append(axis_weights(lowest.astype(jnp.int32), coords - lowest, 8 if i == 0 else 4))
+    starts = jnp.concatenate([cell & 7, (cell >> 3) & 3, cell >> 5], 0).astype(f32)
+    coords = starts + frac_ref[...] + 2.0 * jnp.concatenate(velocity, 0)
+    lowest = jnp.floor(coords)
+    near = coords - lowest
+    base = lowest.astype(jnp.int32)
+    nodes = [outer(near + 1.0), inner(near), inner(1.0 - near), outer(2.0 - near)]
+    weights = [
+        axis_weights(base[i : i + 1, :], [node[i : i + 1, :] for node in nodes], 8 if i == 0 else 4)
+        for i in range(3)
+    ]
     plane = [weights[2][z : z + 1, :] * weights[1][y : y + 1, :] for z in range(4) for y in range(4)]
 
     tiles = grid_ref.shape[0]
@@ -238,37 +236,55 @@
     ids = lax.broadcasted_iota(jnp.int32, (n_dom * tiles, local), 0)
     onehot = jnp.where(ids == tile, 1.0, 0.0).astype(bf16)
     twice = jnp.concatenate([onehot, onehot], 1)
-    dom_copies = []
+    core, chip, chips = lax.rem(dom, 2), dom // 2, n_dom // 2
+    partner = dom + 1 - 2 * core
+    near_copies, far_copies = [], []
     for pair in range(2):
         spread = jnp.concatenate(
             [weights[0] * (plane[k] * carried[2 * pair + c]) for c in range(2) for k in range(16)], 0
         )
-        part_ref[pair] = lax.dot_general(
+        part = lax.dot_general(
             twice,
             jnp.concatenate(split(spread, 2), 1),
             (((1,), (1,)), ((), ())),
             preferred_element_type=f32,
         ).reshape(n_dom, tiles, 256)
-        for step in range(1, n_dom):
-            peer = lax.rem(dom + step, n_dom)
+        for owner in range(n_dom):
+            part_ref[pair, owner % 2, owner // 2] = part[owner]
+        copy = pltpu.make_async_remote_copy(
+            src_ref=part_ref.at[pair, 1 - core],
+            dst_ref=side_ref.at[pair],
+            send_sem=near_send.at[pair],
+            recv_sem=near_recv.at[pair],
+            device_id={"dom": partner},
+            device_id_type=MESH,
+        )
+        copy.start()
+        near_copies.append(copy)
+    for pair in range(2):
+        near_copies[pair].wait_recv()
+        both_ref[pair] = part_ref[pair, core] + side_ref[pair]
+        for step in range(1, chips):
+            peer = lax.rem(chip + step, chips)
             copy = pltpu.make_async_remote_copy(
-                src_ref=part_ref.at[pair, peer],
+                src_ref=both_ref.at[pair, peer],
                 dst_ref=got_ref.at[pair, step],
                 send_sem=dom_send.at[pair, step],
                 recv_sem=dom_recv.at[pair, step],
-                device_id={"dom": peer},
+                device_id={"dom": 2 * peer + core},
                 device_id_type=MESH,
             )
             copy.start()
-            dom_copies.append(copy)
+            far_copies.append(copy)
     for pair in range(2):
-        total = part_ref[pair, dom]
-        for step in range(1, n_dom):
-            dom_copies[pair * (n_dom - 1) + step - 1].wait_recv()
+        for copy in far_copies[pair * (chips - 1) : (pair + 1) * (chips - 1)]:
+            copy.wait_recv()
+        total = both_ref[pair, chip]
+        for step in range(1, chips):
             total = total + got_ref[pair, step]
         for c in range(2):
             grid_ref[:, 2 * pair + c, :] = total[:, 128 * c : 128 * c + 128]
-    for copy in dom_copies:
+    for copy in near_copies + far_copies:
         copy.wait_send()
 
 
@@ -297,9 +313,11 @@
             pltpu.VMEM((64, local), f32),
         ]
         + [pltpu.VMEM((ST, TT), f32)] * 2
-        + [pltpu.VMEM((2, n_dom, tiles, 256), f32)] * 2
+        + [pltpu.VMEM((2, 2, n_dom // 2, tiles, 256), f32)]
+        + [pltpu.VMEM((2, n_dom // 2, tiles, 256), f32)] * 3
         + [pltpu.SemaphoreType.DMA((n_blk,))] * 2
-        + [pltpu.SemaphoreType.DMA((2, n_dom))] * 2,
+        + [pltpu.SemaphoreType.DMA((2, n_dom // 2))] * 2
+        + [pltpu.SemaphoreType.DMA((2,))] * 2,
         compiler_params=pltpu.CompilerParams(collective_id=0, has_side_effects=True, vmem_limit_bytes=56 << 20),
     )(
         positions, strength, core_radius[None], dye_amount[None], cell_fraction, cell_index[None],

time: 90.5 us -> 89.4 us (0.988)
  Pallas kernels: 87.6 us -> 86.5 us
    pallas_call x1, Pallas kernels: 87.6 us -> 86.5 us  [on_device(): pl.pallas_call(functools.partial(step_kernel, n_dom, n_blk), out_shape=(j...]
where the time goes in v5:
time: 89.4 us; the launch traced here: 89.2 us
  Pallas kernels  86.5 us (97%)
  local copies, waits for them, and re-layouts  2 us (2%)
    pallas_call x1, Pallas kernels, on_device(): pl.pallas_call(functools.partial(step_kernel, n_dom, n_blk), out_shape=(j...  86.5 us
    unnamed x4, local copies, waits for them, and re-layouts  2 us

profile of v5, /device:TPU:25, one launch (start us, length us, event | category | flops | bytes accessed | tf_op | source)
XLA Modules:
  0.0 89.2 jit_solution(8097233959134198871)
XLA Ops:
  0.6 86.5 %shard_map.95 = (f32[3,2048]{1,0:T(4,128)}, f32[16,4,128]{2,1,0:T(4,128)}) custom-call(f32[3,2048]{1,0:T(4,128)} %pos_ref.1, f32[3,2048]{1,0:T(4,128)} %str_ref.1, f32[1,2048]{1,0:T(1,128)} %bitcast.5, f32[1,2048]{1,0:T(1,128)} %bitcast.6, f32[3,2048]{1,0:T(4,128)} %frac_ref.1, s32[1,2048]{1,0:T(1,128)} %bitcast.7, s32[1,2048]{1,0:T(1,128)} %bitcast.8, ...), custom_call_target="tpu_custom_call" | custom-call | tf_op jit(solution)/shard_map/pallas_call | solution.py:298
  87.2 0.0 copy-start
  87.2 1.4 %copy.12 = f32[3,2048]{1,0:T(4,128)} copy(f32[3,2048]{1,0:T(4,128)} %get-tuple-element.4) | data formatting | bytes 49152
  88.6 0.0 copy-done
  88.6 0.6 copy.13
Async XLA Ops:
  87.2 1.4 %copy-start = (f32[16,4,128]{2,1,0:T(4,128)S(1)}, f32[16,4,128]{2,1,0:T(4,128)}, u32[]{:S(2)}) copy-start(f32[16,4,128]{2,1,0:T(4,128)} %get-tuple-element.5) | copy-start | bytes 98308

commit v6 on v5

--- a/solution.py
+++ b/solution.py
@@ -43,7 +43,7 @@
     return total
 
 
-TT, ST, PIECE, CHUNK, UNROLL = 256, 512, 128, 32, 16
+TT, ST, PIECE, CHUNK = 256, 512, 128, 32
 
 
 def stack_split(value, parts):
@@ -99,21 +99,15 @@
     qs = (q0, q1)
     chunks = local // ST
     count = chunks * (local // TT)
-    halves = count // UNROLL
-
-    def place_of(index):
-        step = lax.rem(index, count)
-        return (
-            lax.rem(index // count, 2),
-            pl.multiple_of(lax.rem(step, chunks) * ST, ST),
-            pl.multiple_of(step // chunks * TT, TT),
-        )
+
+    def place_of(step):
+        return step % chunks * ST, step // chunks * TT
 
     def squares(index, slot, row):
-        side, start, at = place_of(index)
+        start, at = place_of(index)
         qs[slot][row : row + PIECE, :] = jnp.dot(
-            src_ref[side, pl.ds(pl.multiple_of(start + row, PIECE), PIECE), :],
-            tgt_ref[:, pl.ds(at, TT)],
+            src_ref[start + row : start + row + PIECE, :],
+            tgt_ref[:, at : at + TT],
             preferred_element_type=f32,
         )
 
@@ -129,13 +123,13 @@
             slope_parts += [slope_hi, (slope - slope_hi.astype(f32)).astype(bf16)]
 
     def sums(index, kern_parts, slope_parts):
-        side, start, at = place_of(index)
-        twice = pl.ds(pl.multiple_of(2 * start, 2 * ST), 2 * ST)
-        ok_ref[:, pl.ds(at, TT)] += jnp.dot(
-            rk_ref[side, :, twice], jnp.concatenate(kern_parts, 0), preferred_element_type=f32
-        )
-        og_ref[:, pl.ds(at, TT)] += jnp.dot(
-            rg_ref[side, :, twice], jnp.concatenate(slope_parts, 0), preferred_element_type=f32
+        start, at = place_of(index)
+        twice = slice(2 * start, 2 * start + 2 * ST)
+        ok_ref[:, at : at + TT] += jnp.dot(
+            rk_ref[:, twice], jnp.concatenate(kern_parts, 0), preferred_element_type=f32
+        )
+        og_ref[:, at : at + TT] += jnp.dot(
+            rg_ref[:, twice], jnp.concatenate(slope_parts, 0), preferred_element_type=f32
         )
 
     column = lax.broadcasted_iota(jnp.int32, (128, 256), 1)
@@ -143,7 +137,6 @@
     double = jnp.where(lax.broadcasted_iota(jnp.int32, (128, 256), 0) == origin, 1.0, 0.0).astype(bf16)
 
     def block_tables(block):
-        side = lax.rem(block, 2)
         lead = blocks_ref[block, 0:8, :]
         place = blocks_ref[block, 8:16, :]
         groups = [split(lead if k == 0 else place[k - 1 : k, :] * lead, 2) for k in range(4)]
@@ -159,21 +152,15 @@
             preferred_element_type=f32,
         ).astype(bf16)
         for k in range(local // 128):
-            rk_ref[side, :, 256 * k : 256 * k + 256] = doubled[80 * k : 80 * k + 16]
-            rg_ref[side, :, 256 * k : 256 * k + 256] = doubled[80 * k + 16 : 80 * k + 80]
+            rk_ref[:, 256 * k : 256 * k + 256] = doubled[80 * k : 80 * k + 16]
+            rg_ref[:, 256 * k : 256 * k + 256] = doubled[80 * k + 16 : 80 * k + 80]
         for at in range(0, local, 128):
             s1, s2, s3 = stack_split(place[:, at : at + 128], 3)
-            src_ref[side, at : at + 128, :] = jnp.concatenate([s1, s1, s1, s2, s2, s3], 0).T.astype(bf16)
-
-    block_tables(0)
-    for row in range(0, ST, PIECE):
-        squares(0, 0, row)
-
-    @pl.loop(0, n_blk * halves)
-    def _(part):
-        block = part // halves + 1
-
-        @pl.when((lax.rem(part, halves) == halves - 1) & (block < n_blk))
+            src_ref[at : at + 128, :] = jnp.concatenate([s1, s1, s1, s2, s2, s3], 0).T.astype(bf16)
+
+    @pl.loop(0, n_blk)
+    def _(block):
+        @pl.when(block > 0)
         def _():
             pltpu.make_async_remote_copy(
                 src_ref=blocks_ref.at[0],
@@ -183,14 +170,16 @@
                 device_id={"blk": lax.rem(blk + 1, n_blk)},
                 device_id_type=MESH,
             ).wait_recv()
-            block_tables(block)
-
-        for step in range(UNROLL):
-            index = UNROLL * part + step
-            slot = step % 2
+
+        block_tables(block)
+        for row in range(0, ST, PIECE):
+            squares(0, 0, row)
+        for index in range(count):
+            slot = index % 2
             kern_parts, slope_parts = [], []
             for row in range(0, ST, PIECE):
-                squares(jnp.minimum(index + 1, n_blk * count - 1), 1 - slot, row)
+                if index + 1 < count:
+                    squares(index + 1, 1 - slot, row)
                 values(slot, row, kern_parts, slope_parts)
             sums(index, kern_parts, slope_parts)
 
@@ -306,9 +295,9 @@
         scratch_shapes=[
             pltpu.VMEM((n_blk, 16, local), f32),
             pltpu.VMEM((48, local), bf16),
-            pltpu.VMEM((2, local, 48), bf16),
-            pltpu.VMEM((2, 16, 2 * local), bf16),
-            pltpu.VMEM((2, 64, 2 * local), bf16),
+            pltpu.VMEM((local, 48), bf16),
+            pltpu.VMEM((16, 2 * local), bf16),
+            pltpu.VMEM((64, 2 * local), bf16),
             pltpu.VMEM((16, local), f32),
             pltpu.VMEM((64, local), f32),
         ]

time: 89.4 us -> 82.8 us (0.926)
  Pallas kernels: 86.5 us -> 79.9 us
    pallas_call x1, Pallas kernels: 86.5 us -> 79.9 us  [on_device(): pl.pallas_call(functools.partial(step_kernel, n_dom, n_blk), out_shape=(j...]
where the time goes in v6:
time: 82.8 us; the launch traced here: 82.5 us
  Pallas kernels  79.9 us (96%)
  local copies, waits for them, and re-layouts  2 us (2%)
    pallas_call x1, Pallas kernels, on_device(): pl.pallas_call(functools.partial(step_kernel, n_dom, n_blk), out_shape=(j...  79.9 us
    unnamed x4, local copies, waits for them, and re-layouts  2 us

profile of v6, /device:TPU:25, one launch (start us, length us, event | category | flops | bytes accessed | tf_op | source)
XLA Modules:
  0.0 82.5 jit_solution(13209576129564169471)
XLA Ops:
  0.6 79.9 %shard_map.95 = (f32[3,2048]{1,0:T(4,128)}, f32[16,4,128]{2,1,0:T(4,128)}) custom-call(f32[3,2048]{1,0:T(4,128)} %pos_ref.1, f32[3,2048]{1,0:T(4,128)} %str_ref.1, f32[1,2048]{1,0:T(1,128)} %bitcast.5, f32[1,2048]{1,0:T(1,128)} %bitcast.6, f32[3,2048]{1,0:T(4,128)} %frac_ref.1, s32[1,2048]{1,0:T(1,128)} %bitcast.7, s32[1,2048]{1,0:T(1,128)} %bitcast.8, ...), custom_call_target="tpu_custom_call" | custom-call | tf_op jit(solution)/shard_map/pallas_call | solution.py:287
  80.5 0.0 copy-start
  80.5 1.4 %copy.12 = f32[3,2048]{1,0:T(4,128)} copy(f32[3,2048]{1,0:T(4,128)} %get-tuple-element.4) | data formatting | bytes 49152
  81.9 0.0 copy-done
  81.9 0.6 copy.13
Async XLA Ops:
  80.5 1.4 %copy-start = (f32[16,4,128]{2,1,0:T(4,128)S(1)}, f32[16,4,128]{2,1,0:T(4,128)}, u32[]{:S(2)}) copy-start(f32[16,4,128]{2,1,0:T(4,128)} %get-tuple-element.5) | copy-start | bytes 98308

commit v7 on v6

--- a/solution.py
+++ b/solution.py
@@ -43,7 +43,7 @@
     return total
 
 
-TT, ST, PIECE, CHUNK = 256, 512, 128, 32
+TT, ST, PIECE, CHUNK = 256, 512, 128, 16
 
 
 def stack_split(value, parts):

time: 82.8 us -> 82.3 us (level)
  no operation moved by 1% of the time
where the time goes in v7:
time: 82.3 us; the launch traced here: 82 us
  Pallas kernels  79.4 us (96%)
  local copies, waits for them, and re-layouts  2 us (2%)
    pallas_call x1, Pallas kernels, on_device(): pl.pallas_call(functools.partial(step_kernel, n_dom, n_blk), out_shape=(j...  79.4 us
    unnamed x4, local copies, waits for them, and re-layouts  2 us

profile of v7, /device:TPU:25, one launch (start us, length us, event | category | flops | bytes accessed | tf_op | source)
XLA Modules:
  0.0 82.0 jit_solution(15617614619500783880)
XLA Ops:
  0.6 79.4 %shard_map.95 = (f32[3,2048]{1,0:T(4,128)}, f32[16,4,128]{2,1,0:T(4,128)}) custom-call(f32[3,2048]{1,0:T(4,128)} %pos_ref.1, f32[3,2048]{1,0:T(4,128)} %str_ref.1, f32[1,2048]{1,0:T(1,128)} %bitcast.5, f32[1,2048]{1,0:T(1,128)} %bitcast.6, f32[3,2048]{1,0:T(4,128)} %frac_ref.1, s32[1,2048]{1,0:T(1,128)} %bitcast.7, s32[1,2048]{1,0:T(1,128)} %bitcast.8, ...), custom_call_target="tpu_custom_call" | custom-call | tf_op jit(solution)/shard_map/pallas_call | solution.py:287
  80.0 0.0 copy-start
  80.0 1.4 %copy.12 = f32[3,2048]{1,0:T(4,128)} copy(f32[3,2048]{1,0:T(4,128)} %get-tuple-element.4) | data formatting | bytes 49152
  81.4 0.0 copy-done
  81.4 0.6 copy.13
Async XLA Ops:
  80.0 1.4 %copy-start = (f32[16,4,128]{2,1,0:T(4,128)S(1)}, f32[16,4,128]{2,1,0:T(4,128)}, u32[]{:S(2)}) copy-start(f32[16,4,128]{2,1,0:T(4,128)} %get-tuple-element.5) | copy-start | bytes 98308
